TPU v7x, 128 devices: a whole 4x4x4 slice. The times are simulated.
128 devices in a mesh: row: 4 (over y), col: 32 (over x, z, core).
Axes of the slice: x: 4, y: 4, z: 4, core: 2. Of those that a mesh axis runs over, the one named last changes fastest.
Arguments:
- coordinates: float32 [3, 65536], replicated, may hold values from 0 to 1
- ordering: int32 [65536], replicated, may hold values from 0 to 65535, each once
- neighbours: int32 [256, 4], replicated, may hold values from 0 to 254, as said below
- cross: float32 [256, 4, 256, 256], P(('row', 'col')), may hold values from -0.1875 to 0.1875
- whitening: float32 [256, 256, 256], P(('row', 'col')), may hold values from -0.1875 to 0.1875
- solution: float32 [256, 8, 256], P(('row', 'col')), may hold values from -6 to 6
- residual: float32 [256, 8, 256], P(('row', 'col')), may hold values from -40 to 40
- direction: float32 [256, 8, 256], P(('row', 'col')), may hold values from -40 to 40
Outputs:
- solution_next: float32 [256, 8, 256], P(('row', 'col'))
- residual_next: float32 [256, 8, 256], P(('row', 'col'))
- direction_next: float32 [256, 8, 256], P(('row', 'col'))
Inputs may be any that keep to these rules, and one draw needn't show every extreme that they name: `neighbours`: row b lists b - 1 first, then further distinct blocks below b - 1; where fewer than 4 earlier blocks exist the remaining entries equal b itself.
All inputs are finite; a program needn't handle non-finite values.
Results may differ from a plain program's by a relative error of at most 0.00023.
Values sent between devices are 32-bit elements; how exact they have to be, the bound alone decides.
No kernel may reach another device: no remote copies, remote signals or barrier semaphores. Data moves between devices by JAX's collectives and lax.ppermute only.
A program may use at most 192 MiB of HBM per device.

v0:
```python
import functools
import math

import jax
import jax.numpy as jnp
from jax import lax
from jax.experimental import pallas as pl
from jax.experimental.pallas import tpu as pltpu
from jax.sharding import PartitionSpec as P

f32 = jnp.float32
bf16 = jnp.bfloat16
highest = lax.Precision.HIGHEST
rate = math.sqrt(3.0) / 0.3 * math.log2(math.e)
offset = 1.0 / math.log(2.0)
variance = 0.05 * math.log(2.0)
nugget = 1.0
AXES = ("row", "col")
BS, RHS, NBR, OWN = 256, 8, 4, 2
HALF = 128
STEP = 4
PEERS = 64
MEGA = 1 << 20


def dot(a, b, dims):
    return lax.dot_general(a, b, (dims, ((), ())), precision=highest, preferred_element_type=f32)


def split2(v):
    top = v.astype(bf16)
    return top, (v - top.astype(f32)).astype(bf16)


def split3(v):
    top = v.astype(bf16).astype(f32)
    rest = v - top
    middle = rest.astype(bf16).astype(f32)
    return top, middle, rest - middle


def features(place, own):
    a = (place - 0.5) * rate
    norm = jnp.sum(a * a, axis=0, keepdims=True)
    one = jnp.ones_like(norm)
    pad = jnp.zeros((3, norm.shape[1]), f32)
    parts = [-2.0 * a, one, norm, pad] if own else [a, norm, one, pad]
    top, middle, low = split3(jnp.concatenate(parts, axis=0))
    order = [top, middle, top, middle, low, top] if own else [top, top, middle, middle, top, low]
    return jnp.concatenate(order, axis=0).astype(bf16)


def places(tiles, block):
    rows = slice(3 * block, 3 * block + 3)
    return jnp.concatenate([tiles[4, rows, :], tiles[5, rows, :]], axis=1)


def pick_points(order_ref, coordinates_ref, direction_ref, out_ref):
    lane = lax.broadcasted_iota(jnp.int32, (3, HALF), 1)
    groups = 2 * OWN

    def one_point(i, found):
        kept = []
        for group in range(groups):
            at = order_ref[group * HALF + i]
            base = pl.multiple_of((at >> 7) << 7, HALF)
            line = coordinates_ref[:, pl.ds(base, HALF)]
            turned = pltpu.roll(line, (i - (at & (HALF - 1))) & (HALF - 1), 1)
            kept.append(jnp.where(lane == i, turned, found[group]))
        return tuple(kept)

    found = lax.fori_loop(0, HALF, one_point, (jnp.zeros((3, HALF), f32),) * groups, unroll=4)
    pad = jnp.zeros((2, HALF), f32)
    tiles = []
    for block in range(OWN):
        for half in range(2):
            tiles.append(direction_ref[block, :, half * HALF : (half + 1) * HALF])
    for half in range(2):
        tiles.append(jnp.concatenate([found[half], found[2 + half], pad], axis=0))

    def copy(i, carry):
        for part, tile in enumerate(tiles):
            out_ref[i, part] = tile
        return carry

    lax.fori_loop(0, out_ref.shape[0], copy, 0)


def point_payload(own_order, coordinates, direction, copies):
    return pl.pallas_call(
        pick_points,
        out_shape=jax.ShapeDtypeStruct((copies, 6, RHS, HALF), f32),
        in_specs=[
            pl.BlockSpec(memory_space=pltpu.SMEM),
            pl.BlockSpec(memory_space=pltpu.VMEM),
            pl.BlockSpec(memory_space=pltpu.VMEM),
        ],
        out_specs=pl.BlockSpec(memory_space=pltpu.VMEM),
        compiler_params=pltpu.CompilerParams(vmem_limit_bytes=8 * MEGA),
        name="pick_points",
    )(own_order, coordinates, direction)


TALL, WIDE = 512, 256


def image_kernel(pieces, own_ref, start_ref, *refs):
    columns, (out_ref, own_part, column_part, field_part, square) = refs[:pieces], refs[pieces:]
    each = pl.num_programs(0) // pieces

    @pl.when(pl.program_id(0) == 0)
    def _():
        for block in range(OWN):
            own_part[:, block * BS : (block + 1) * BS] = features(places(own_ref, block), True)
        out_ref[...] = start_ref[...]

    def prepare(columns_ref):
        for member in range(STEP):
            for block in range(OWN):
                at = OWN * member + block
                tiles = columns_ref.at[member]
                column_part[at * BS : (at + 1) * BS, :] = features(places(tiles, block), False).T
                field = jnp.concatenate([tiles[2 * block], tiles[2 * block + 1]], axis=1)
                field_part[at] = jnp.concatenate(split2(field * variance), axis=0)

    for index, columns_ref in enumerate(columns):
        pl.when(pl.program_id(0) // each == index)(functools.partial(prepare, columns_ref))
    jobs = [
        (q, r) for r in range(OWN * BS // WIDE) for q in range(STEP * OWN * BS // TALL)
    ]

    def fill(job, slot):
        q, r = jobs[job]
        square[slot] = jnp.dot(
            column_part[q * TALL : (q + 1) * TALL, :],
            own_part[:, r * WIDE : (r + 1) * WIDE],
            preferred_element_type=f32,
        )

    fill(0, 0)
    for job, (q, r) in enumerate(jobs):
        if job + 1 < len(jobs):
            fill(job + 1, (job + 1) % 2)
        for part in range(TALL // BS):
            for lanes in range(WIDE // HALF):
                x = square[
                    job % 2, part * BS : (part + 1) * BS, lanes * HALF : (lanes + 1) * HALF
                ]
                x = jnp.maximum(x, 1e-30)
                t = x * lax.rsqrt(x)
                tile = (t + offset) * jnp.exp2(-t)
                top, low = split2(tile)
                field = field_part[q * (TALL // BS) + part]
                where = slice(r * WIDE + lanes * HALF, r * WIDE + (lanes + 1) * HALF)
                out_ref[:, where] += jnp.dot(
                    field, top, preferred_element_type=f32
                ) + jnp.dot(field, low, preferred_element_type=f32)


def add_image(own, columns, start):
    pieces, count = len(columns), columns[0].shape[0]
    each = count // STEP
    pairs = pieces * count * OWN * BS * OWN * BS

    def piece_spec(index):
        return pl.BlockSpec(
            (STEP, 6, RHS, HALF),
            lambda i: (jnp.clip(i - index * each, 0, each - 1), 0, 0, 0),
        )

    return pl.pallas_call(
        functools.partial(image_kernel, pieces),
        grid=(pieces * each,),
        in_specs=[
            pl.BlockSpec((6, RHS, HALF), lambda i: (0, 0, 0)),
            pl.BlockSpec((2 * RHS, OWN * BS), lambda i: (0, 0)),
        ]
        + [piece_spec(index) for index in range(pieces)],
        out_specs=pl.BlockSpec((2 * RHS, OWN * BS), lambda i: (0, 0)),
        out_shape=jax.ShapeDtypeStruct((2 * RHS, OWN * BS), f32),
        scratch_shapes=[
            pltpu.VMEM((48, OWN * BS), bf16),
            pltpu.VMEM((STEP * OWN * BS, 48), bf16),
            pltpu.VMEM((OWN * STEP, 2 * RHS, BS), bf16),
            pltpu.VMEM((2, TALL, WIDE), f32),
        ],
        compiler_params=pltpu.CompilerParams(vmem_limit_bytes=24 * MEGA),
        cost_estimate=pl.CostEstimate(
            flops=600 * pairs, transcendentals=2 * pairs, bytes_accessed=pieces * count * 6 * 4096
        ),
        name="image",
    )(own, start, *columns)


def lower(near, valid_ref, cross_ref, field, block):
    total = field
    for k in range(NBR):
        weight = valid_ref[block * NBR + k].astype(f32)
        total = total - dot(near(block, k) * weight, cross_ref[block, k], ((1,), (1,)))
    return total


def whiten_of(whitening_ref, block):
    rows = lax.broadcasted_iota(jnp.int32, (BS, BS), 0)
    lanes = lax.broadcasted_iota(jnp.int32, (BS, BS), 1)
    return whitening_ref[block] + jnp.where(rows == lanes, 1.0, 0.0)


def lanes_of(v):
    return v[:, :HALF] + v[:, HALF:]


def measure_kernel(
    list_ref, valid_ref, all_ref, residual_ref, cross_ref, whitening_ref, sum_ref, direction_ref,
    out_ref, near_ref, near_buf, sems,
):
    copies = []
    for b in range(OWN):
        for k in range(NBR):
            at = b * NBR + k
            copies.append(
                pltpu.make_async_copy(all_ref.at[list_ref[at]], near_buf.at[at], sems.at[at])
            )
            copies[-1].start()
    for copy in copies:
        copy.wait()
    old = jnp.zeros((RHS, HALF), f32)
    curvature = jnp.zeros((RHS, HALF), f32)
    tiles = []
    for b in range(OWN):
        lowered = lower(
            lambda b, k: near_buf[b * NBR + k], valid_ref, cross_ref, residual_ref[b], b
        )
        mapped = dot(lowered, whiten_of(whitening_ref, b), ((1,), (1,)))
        old = old + lanes_of(mapped * mapped)
        here = slice(b * BS, (b + 1) * BS)
        image = sum_ref[:RHS, here] + sum_ref[RHS:, here] + nugget * direction_ref[b]
        curvature = curvature + lanes_of(direction_ref[b] * image)
        tiles += [image[:, :HALF], image[:, HALF:]]
    lane = lax.broadcasted_iota(jnp.int32, (RHS, HALF), 1)
    old = jnp.sum(old, axis=1, keepdims=True)
    curvature = jnp.sum(curvature, axis=1, keepdims=True)
    tiles.append(jnp.where(lane == 0, old, jnp.where(lane == 1, curvature, 0.0)))

    def copy(i, carry):
        for part, tile in enumerate(tiles):
            out_ref[i, part] = tile
        return carry

    lax.fori_loop(0, out_ref.shape[0], copy, 0)
    near_ref[...] = near_buf[...]


def measure_step(lists, valid, gathered, residual, cross, whitening, total, direction):
    smem = pl.BlockSpec(memory_space=pltpu.SMEM)
    vmem = pl.BlockSpec(memory_space=pltpu.VMEM)
    return pl.pallas_call(
        measure_kernel,
        out_shape=(
            jax.ShapeDtypeStruct((PEERS, 5, RHS, HALF), f32),
            jax.ShapeDtypeStruct((OWN * NBR, RHS, BS), f32),
        ),
        in_specs=[smem, smem, pl.BlockSpec(memory_space=pl.ANY), vmem, vmem, vmem, vmem, vmem],
        out_specs=(vmem, vmem),
        scratch_shapes=[
            pltpu.VMEM((OWN * NBR, RHS, BS), f32),
            pltpu.SemaphoreType.DMA((OWN * NBR,)),
        ],
        compiler_params=pltpu.CompilerParams(vmem_limit_bytes=24 * MEGA),
        name="measure_step",
    )(lists, valid, gathered, residual, cross, whitening, total, direction)


def spread_kernel(
    at_ref, valid_ref, into_ref, self_ref, mine_ref, other_ref, near_ref, residual_ref, solution_ref,
    direction_ref, cross_ref, whitening_ref,
    solution_out, residual_out, scaled_out, out_ref, old_out,
):
    total = jnp.zeros((RHS, HALF), f32)
    for i in range(PEERS):
        total = total + mine_ref[i, 4] + other_ref[i, 4]
    old = total[:, 0:1]
    step = old / total[:, 1:2]

    def clear(i, carry):
        for part in range(2 * OWN):
            out_ref[i, part] = jnp.zeros((RHS, HALF), f32)
        return carry

    lax.fori_loop(0, 2 * PEERS, clear, 0)

    def image_of(at):
        slot = at & 63
        a = jnp.concatenate([mine_ref[slot, 2 * (at >> 7)], mine_ref[slot, 2 * (at >> 7) + 1]], 1)
        b = jnp.concatenate([other_ref[slot, 2 * (at >> 7)], other_ref[slot, 2 * (at >> 7) + 1]], 1)
        return jnp.where(((at >> 6) & 1) == 0, a, b)

    newer = jnp.zeros((RHS, HALF), f32)
    for b in range(OWN):
        solution_out[b] = solution_ref[b] + step * direction_ref[b]
        image = jnp.concatenate(
            [mine_ref[self_ref[0], 2 * b], mine_ref[self_ref[0], 2 * b + 1]], 1
        )
        following = residual_ref[b] - step * image
        residual_out[b] = following
        lowered = lower(
            lambda b, k: near_ref[b * NBR + k] - step * image_of(at_ref[b * NBR + k]),
            valid_ref, cross_ref, following, b,
        )
        whiten = whiten_of(whitening_ref, b)
        mapped = dot(lowered, whiten, ((1,), (1,)))
        newer = newer + lanes_of(mapped * mapped)
        scaled = dot(mapped, whiten, ((1,), (0,)))
        scaled_out[b] = scaled
        for k in range(NBR):
            at = b * NBR + k
            spread = dot(scaled, cross_ref[b, k], ((1,), (0,))) * valid_ref[at].astype(f32)
            to = into_ref[at]
            out_ref[to >> 1, 2 * (to & 1)] += spread[:, :HALF]
            out_ref[to >> 1, 2 * (to & 1) + 1] += spread[:, HALF:]
    newer = jnp.sum(newer, axis=1, keepdims=True)
    lane = lax.broadcasted_iota(jnp.int32, (RHS, HALF), 1)
    newer = jnp.where(lane == 0, newer, 0.0)

    def share(i, carry):
        out_ref[i, 2 * OWN] = newer
        return carry

    lax.fori_loop(0, 2 * PEERS, share, 0)
    old_out[...] = jnp.broadcast_to(old, (RHS, HALF))


def sum_kernel(all_ref, scaled_ref, direction_ref, old_ref, out_ref):
    total = all_ref[0]
    for i in range(1, PEERS):
        total = total + all_ref[i]
    ratio = total[2 * OWN, :, 0:1] / old_ref[:, 0:1]
    for b in range(OWN):
        back = jnp.concatenate([total[2 * b], total[2 * b + 1]], axis=1)
        out_ref[b] = scaled_ref[b] - back + ratio * direction_ref[b]


def sum_step(everything, scaled, direction, old):
    vmem = pl.BlockSpec(memory_space=pltpu.VMEM)
    return pl.pallas_call(
        sum_kernel,
        out_shape=jax.ShapeDtypeStruct((OWN, RHS, BS), f32),
        in_specs=[vmem] * 4,
        out_specs=vmem,
        compiler_params=pltpu.CompilerParams(vmem_limit_bytes=8 * MEGA),
        name="sum_step",
    )(everything, scaled, direction, old)


def spread_step(
    at, valid, into, self_at, mine, other, near, residual, solution, direction, cross, whitening
):
    smem = pl.BlockSpec(memory_space=pltpu.SMEM)
    vmem = pl.BlockSpec(memory_space=pltpu.VMEM)
    own = jax.ShapeDtypeStruct((OWN, RHS, BS), f32)
    return pl.pallas_call(
        spread_kernel,
        out_shape=(
            own,
            own,
            own,
            jax.ShapeDtypeStruct((2 * PEERS, 2 * OWN + 1, RHS, HALF), f32),
            jax.ShapeDtypeStruct((RHS, HALF), f32),
        ),
        in_specs=[smem] * 4 + [vmem] * 8,
        out_specs=(vmem,) * 5,
        compiler_params=pltpu.CompilerParams(vmem_limit_bytes=40 * MEGA),
        name="spread_step",
    )(
        at, valid, into, self_at, mine, other, near, residual, solution, direction, cross,
        whitening,
    )


def x_around(hop):
    def target(i):
        return (i // 8 + hop) % 4 * 8 + i % 8

    return functools.partial(
        lax.ppermute, axis_name="col", perm=[(i, target(i)) for i in range(32)]
    )


def to_other_core(value):
    return lax.ppermute(value, "col", [(i, i ^ 1) for i in range(32)])


def exchange(value, groups):
    return lax.all_to_all(value, AXES, 0, 0, axis_index_groups=groups, tiled=True)


SAME_CORE = [[2 * j + core for j in range(PEERS)] for core in range(2)]
SAME_X = [
    [y * 32 + x * 8 + z * 2 + core for core in range(2) for y in range(4) for z in range(4)]
    for x in range(4)
]


def per_device(coordinates, ordering, neighbours, cross, whitening, solution, residual, direction):
    row = lax.axis_index("row")
    col = lax.axis_index("col")
    device = row * 32 + col
    here_core = device % 2
    own_ids = device * OWN + jnp.arange(OWN, dtype=jnp.int32)
    own_lists = lax.dynamic_slice_in_dim(neighbours, device * OWN, OWN, 0)
    valid = (own_lists < own_ids[:, None]).astype(jnp.int32).reshape(-1)
    lists = own_lists.reshape(-1)
    their = lists // OWN
    core_gap = (their % 2) ^ here_core
    at = ((lists % OWN) * 2 + core_gap) * PEERS + their // 2
    into = (core_gap * PEERS + their // 2) * OWN + lists % OWN
    self_at = (device // 2)[None]

    gathered = lax.all_gather(residual, AXES, axis=0, tiled=True)

    own_order = lax.dynamic_slice_in_dim(ordering, device * (OWN * BS), OWN * BS, 0)
    payload = point_payload(own_order, coordinates, direction, 32)
    own = payload[0]
    plane = exchange(payload, SAME_X)
    half = plane.shape[0] // 2
    same = jnp.where(here_core == 0, plane[:half], plane[half:])
    beyond = [x_around(hop)(same) for hop in (1, 3, 2)]
    total = add_image(own, [plane], jnp.zeros((2 * RHS, OWN * BS), f32))
    others = [to_other_core(piece) for piece in beyond]
    total = add_image(own, beyond, total)
    total = add_image(own, others, total)

    image, near = measure_step(
        lists, valid, gathered, residual, cross, whitening, total, direction
    )
    mine = exchange(image, SAME_CORE)
    other = to_other_core(mine)
    solution_next, residual_next, scaled, back, old = spread_step(
        at, valid, into, self_at, mine, other, near, residual, solution, direction, cross,
        whitening,
    )
    back = back[:PEERS] + to_other_core(back[PEERS:])
    direction_next = sum_step(exchange(back, SAME_CORE), scaled, direction, old)
    return (solution_next, residual_next, direction_next)


def solution(mesh):
    placed = (
        P(),
        P(),
        P(),
        P(("row", "col"), None, None, None),
        P(("row", "col"), None, None),
        P(("row", "col"), None, None),
        P(("row", "col"), None, None),
        P(("row", "col"), None, None),
    )
    return jax.shard_map(
        per_device,
        mesh=mesh,
        in_specs=placed,
        out_specs=(
            P(("row", "col"), None, None),
            P(("row", "col"), None, None),
            P(("row", "col"), None, None),
        ),
        check_vma=False,
    )
```

profile of v0, /device:TPU:0, one launch (start us, length us, event | category | flops | bytes accessed | tf_op | source)
XLA Modules:
  0.0 196.1 jit_solution(6587231285324164443)
XLA Ops:
  7.2 0.7 all-gather.2.cloned.1.call-update
  7.9 0.8 dynamic_slice.7.order_ref
  8.7 1.2 copy-done.4
  9.9 0.7 copy-done.5
  10.6 5.0 %pick_points.1 = f32[32,6,8,128]{3,2,1,0:T(8,128)} custom-call(s32[512]{0:T(512)S(1)} %dynamic_slice.7.order_ref, f32[3,65536]{1,0:T(4,128)S(1)} %copy-done.4, f32[2,8,256]{2,1,0:T(8,128)S(1)} %copy-done.5), custom_call_target="tpu_custom_call" | custom-call | tf_op jit(solution)/shard_map/pick_points/pallas_call | solution.py:90
  15.6 8.4 %all-to-all-start = ((f32[32,6,8,128]{3,2,1,0:T(8,128)}), f32[32,6,8,128]{3,2,1,0:T(8,128)S(1)}, u32[]{:S(2)}, u32[]{:S(2)}) async-start(f32[32,6,8,128]{3,2,1,0:T(8,128)} %pick_points.1), calls=%async_computation | async-start | bytes 1572864 | tf_op jit(solution)/shard_map/all_to_all | solution.py:394
  24.5 0.7 slice_bitcast_fusion.own_ref
  25.2 13.6 %all-to-all-done.refs_0_ = f32[32,6,8,128]{3,2,1,0:T(8,128)S(1)} async-done(((f32[32,6,8,128]{3,2,1,0:T(8,128)}), f32[32,6,8,128]{3,2,1,0:T(8,128)S(1)}, u32[]{:S(2)}, u32[]{:S(2)}) %all-to-all-start) | async-done | bytes 786464 | tf_op jit(solution)/shard_map/all_to_all | solution.py:394
  38.9 3.1 %collective-permute-start.2 = (f32[16,6,8,128]{3,2,1,0:T(8,128)S(1)}, f32[16,6,8,128]{3,2,1,0:T(8,128)S(1)}, u32[]{:S(2)}, u32[]{:S(2)}) collective-permute-start(f32[16,6,8,128]{3,2,1,0:T(8,128)S(1)} %slice_select_fusion), channel_id=1, source_target_pairs={{0,16},{1,17},{2,18},{3,19},{4,20},{5,21},{6,22},{7,23},{8,24},{9,... | collective-permute-start | bytes 1179656 | tf_op jit(solution)/shard_map/ppermute | solution.py:427
  42.0 1.1 collective-permute-start.1
  43.1 0.9 collective-permute-start
  44.0 17.1 %image.3.start_ref = f32[16,512]{1,0:T(8,128)S(1)} custom-call(f32[6,8,128]{2,1,0:T(8,128)S(1)} %slice_bitcast_fusion.own_ref, f32[16,512]{1,0:T(8,128)S(1)} %broadcast_in_dim.8.start_ref, f32[32,6,8,128]{3,2,1,0:T(8,128)S(1)} %all-to-all-done.refs_0_), custom_call_target="tpu_custom_call" | custom-call | flops 5033164800 | bytes 786432 | tf_op jit(solution)/shard_map/image/pallas_call | solution.py:171
  61.2 0.5 collective-permute-start.4
  61.8 25.7 %image.4.start_ref = f32[16,512]{1,0:T(8,128)S(1)} custom-call(f32[6,8,128]{2,1,0:T(8,128)S(1)} %slice_bitcast_fusion.own_ref, f32[16,512]{1,0:T(8,128)S(1)} %image.3.start_ref, f32[16,6,8,128]{3,2,1,0:T(8,128)S(1)} %collective-permute-done.refs_0_, f32[16,6,8,128]{3,2,1,0:T(8,128)S(1)} %collective-permute-done.1.refs_1_, ...), custom_call_target="tpu_custom_call" | custom-call | flops 7549747200 | bytes 1179648 | tf_op jit(solution)/shard_map/image/pallas_call | solution.py:171
  87.6 25.6 %image.5.sum_ref = f32[16,512]{1,0:T(8,128)S(1)} custom-call(f32[6,8,128]{2,1,0:T(8,128)S(1)} %slice_bitcast_fusion.own_ref, f32[16,512]{1,0:T(8,128)S(1)} %image.4.start_ref, f32[16,6,8,128]{3,2,1,0:T(8,128)S(1)} %collective-permute-done.3.refs_0_, f32[16,6,8,128]{3,2,1,0:T(8,128)S(1)} %collective-permute-done.4.refs_1_, ...), custom_call_target="tpu_custom_call" | custom-call | flops 7549747200 | bytes 1179648 | tf_op jit(solution)/shard_map/image/pallas_call | solution.py:171
  113.3 1.6 copy-done.1
  114.9 3.8 %measure_step.1 = (f32[64,5,8,128]{3,2,1,0:T(8,128)S(1)}, f32[8,8,256]{2,1,0:T(8,128)S(1)}) custom-call(s32[8]{0:T(128)S(1)} %reshape.18.list_ref, s32[8]{0:T(128)S(1)} %reshape.22.valid_ref, f32[256,8,256]{2,1,0:T(8,128)S(1)} %copy-done.1, f32[2,8,256]{2,1,0:T(8,128)S(1)} %copy-done.7, f32[2,4,256,256]{3,2,1,0:T(8,128)S(1)} %copy-done, ...), custom_call_target="tpu_custom_call" | custom-call | tf_op jit(solution)/shard_map/measure_step/pallas_call | solution.py:257
  118.7 27.9 %all_to_all.15.mine_ref = f32[64,5,8,128]{3,2,1,0:T(8,128)S(1)} all-to-all(f32[64,5,8,128]{3,2,1,0:T(8,128)S(1)} %get-tuple-element.10), channel_id=1, replica_groups={{0,2,4,6,8,10,12,14,16,18,20,22,24,26,28,30,32,34,36,38,40,42,44,46,48,..., dimensions={0} | all-to-all | bytes 2621440 | tf_op jit(solution)/shard_map/all_to_all | solution.py:394
  146.6 3.1 %collective-permute-done.6.other_ref = f32[64,5,8,128]{3,2,1,0:T(8,128)} collective-permute-done((f32[64,5,8,128]{3,2,1,0:T(8,128)S(1)}, f32[64,5,8,128]{3,2,1,0:T(8,128)}, u32[]{:S(2)}, u32[]{:S(2)}) %collective-permute-start.6) | collective-permute-done | bytes 1310752 | tf_op jit(solution)/shard_map/ppermute | solution.py:390
  149.7 1.0 copy-done.3
  150.8 7.9 %spread_step.1 = (f32[2,8,256]{2,1,0:T(8,128)}, f32[2,8,256]{2,1,0:T(8,128)}, f32[2,8,256]{2,1,0:T(8,128)S(1)}, f32[128,5,8,128]{3,2,1,0:T(8,128)S(1)}, f32[8,128]{1,0:T(8,128)S(1)}) custom-call(s32[8]{0:T(128)S(1)} %multiply_add_fusion.1.at_ref, s32[8]{0:T(128)S(1)} %reshape.22.valid_ref, s32[8]{0:T(128)S(1)} %get-tuple-element.17.into_ref, ...), custom_call_target="tpu_custom_call" | custom-call | tf_op jit(solution)/shard_map/spread_step/pallas_call | solution.py:361
  158.9 2.9 %collective-permute-done.7 = f32[64,5,8,128]{3,2,1,0:T(8,128)S(1)} collective-permute-done((f32[64,5,8,128]{3,2,1,0:T(8,128)S(1)}, f32[64,5,8,128]{3,2,1,0:T(8,128)S(1)}, u32[]{:S(2)}, u32[]{:S(2)}) %collective-permute-start.7) | collective-permute-done | bytes 1310752 | tf_op jit(solution)/shard_map/ppermute | solution.py:390
  162.0 26.6 %all_to_all.16.all_ref = f32[64,5,8,128]{3,2,1,0:T(8,128)S(1)} all-to-all(f32[64,5,8,128]{3,2,1,0:T(8,128)S(1)} %slice_add_fusion), channel_id=1, replica_groups={{0,2,4,6,8,10,12,14,16,18,20,22,24,26,28,30,32,34,36,38,40,42,44,46,48,..., dimensions={0} | all-to-all | bytes 2621440 | tf_op jit(solution)/shard_map/all_to_all | solution.py:394
  188.5 0.7 sum_step.1
  (41 shorter events, 1.3 us)
Async XLA Ops:
  7.2 106.1 %all-gather.2.cloned.1.call-start = ((), (), s32[]{:S(2)}) async-start(), calls=%async_computation.3 | async-start | bytes 2113536 | tf_op jit(solution)/shard_map/all_gather | solution.py:419
  8.7 1.2 copy-start.4
  9.9 0.7 copy-start.5
  10.6 13.4 %copy-start.9 = (s32[256,4]{0,1:T(4,128)S(1)}, s32[256,4]{0,1:T(4,128)}, u32[]{:S(2)}) copy-start(s32[256,4]{0,1:T(4,128)} %param.10) | copy-start | bytes 12292
  15.6 23.3 %all-to-all-start = ((f32[32,6,8,128]{3,2,1,0:T(8,128)}), f32[32,6,8,128]{3,2,1,0:T(8,128)S(1)}, u32[]{:S(2)}, u32[]{:S(2)}) async-start(f32[32,6,8,128]{3,2,1,0:T(8,128)} %pick_points.1), calls=%async_computation | async-start | bytes 1572864 | tf_op jit(solution)/shard_map/all_to_all | solution.py:394
  38.9 22.2 %collective-permute-start.2 = (f32[16,6,8,128]{3,2,1,0:T(8,128)S(1)}, f32[16,6,8,128]{3,2,1,0:T(8,128)S(1)}, u32[]{:S(2)}, u32[]{:S(2)}) collective-permute-start(f32[16,6,8,128]{3,2,1,0:T(8,128)S(1)} %slice_select_fusion), channel_id=1, source_target_pairs={{0,16},{1,17},{2,18},{3,19},{4,20},{5,21},{6,22},{7,23},{8,24},{9,... | collective-permute-start | bytes 1179656 | tf_op jit(solution)/shard_map/ppermute | solution.py:427
  42.0 19.2 %collective-permute-start.1 = (f32[16,6,8,128]{3,2,1,0:T(8,128)S(1)}, f32[16,6,8,128]{3,2,1,0:T(8,128)S(1)}, u32[]{:S(2)}, u32[]{:S(2)}) collective-permute-start(f32[16,6,8,128]{3,2,1,0:T(8,128)S(1)} %slice_select_fusion), channel_id=1, source_target_pairs={{0,24},{1,25},{2,26},{3,27},{4,28},{5,29},{6,30},{7,31},{8,0},{9,1... | collective-permute-start | bytes 1179656 | tf_op jit(solution)/shard_map/ppermute | solution.py:427
  43.1 18.6 %collective-permute-start = (f32[16,6,8,128]{3,2,1,0:T(8,128)S(1)}, f32[16,6,8,128]{3,2,1,0:T(8,128)S(1)}, u32[]{:S(2)}, u32[]{:S(2)}) collective-permute-start(f32[16,6,8,128]{3,2,1,0:T(8,128)S(1)} %slice_select_fusion), channel_id=1, source_target_pairs={{0,8},{1,9},{2,10},{3,11},{4,12},{5,13},{6,14},{7,15},{8,16},{9,17... | collective-permute-start | bytes 1179656 | tf_op jit(solution)/shard_map/ppermute | solution.py:427
  61.1 26.4 %collective-permute-start.5 = (f32[16,6,8,128]{3,2,1,0:T(8,128)S(1)}, f32[16,6,8,128]{3,2,1,0:T(8,128)S(1)}, u32[]{:S(2)}, u32[]{:S(2)}) collective-permute-start(f32[16,6,8,128]{3,2,1,0:T(8,128)S(1)} %collective-permute-done.2.refs_2_), channel_id=1, source_target_pairs={{0,1},{1,0},{2,3},{3,2},{4,5},{5,4},{6,7},{7,6},{8,9},{9,8},{10,11... | collective-permute-start | bytes 1179656 | tf_op jit(solution)/shard_map/ppermute | solution.py:390
  61.2 26.3 %collective-permute-start.4 = (f32[16,6,8,128]{3,2,1,0:T(8,128)S(1)}, f32[16,6,8,128]{3,2,1,0:T(8,128)S(1)}, u32[]{:S(2)}, u32[]{:S(2)}) collective-permute-start(f32[16,6,8,128]{3,2,1,0:T(8,128)S(1)} %collective-permute-done.1.refs_1_), channel_id=1, source_target_pairs={{0,1},{1,0},{2,3},{3,2},{4,5},{5,4},{6,7},{7,6},{8,9},{9,8},{10,11... | collective-permute-start | bytes 1179656 | tf_op jit(solution)/shard_map/ppermute | solution.py:390
  61.7 25.8 %collective-permute-start.3 = (f32[16,6,8,128]{3,2,1,0:T(8,128)S(1)}, f32[16,6,8,128]{3,2,1,0:T(8,128)S(1)}, u32[]{:S(2)}, u32[]{:S(2)}) collective-permute-start(f32[16,6,8,128]{3,2,1,0:T(8,128)S(1)} %collective-permute-done.refs_0_), channel_id=1, source_target_pairs={{0,1},{1,0},{2,3},{3,2},{4,5},{5,4},{6,7},{7,6},{8,9},{9,8},{10,11... | collective-permute-start | bytes 1179656 | tf_op jit(solution)/shard_map/ppermute | solution.py:390
  87.5 25.7 %copy-start.2 = (f32[2,256,256]{2,1,0:T(8,128)S(1)}, f32[2,256,256]{2,1,0:T(8,128)}, u32[]{:S(2)}) copy-start(f32[2,256,256]{2,1,0:T(8,128)} %whitening_ref.3) | copy-start | bytes 1572868
  87.5 25.7 %copy-start.6 = (f32[2,8,256]{2,1,0:T(8,128)S(1)}, f32[2,8,256]{2,1,0:T(8,128)}, u32[]{:S(2)}) copy-start(f32[2,8,256]{2,1,0:T(8,128)} %direction_ref.7) | copy-start | bytes 49156
  87.5 25.7 %copy-start.7 = (f32[2,8,256]{2,1,0:T(8,128)S(1)}, f32[2,8,256]{2,1,0:T(8,128)}, u32[]{:S(2)}) copy-start(f32[2,8,256]{2,1,0:T(8,128)} %residual_ref.3) | copy-start | bytes 49156
  87.6 25.7 %copy-start = (f32[2,4,256,256]{3,2,1,0:T(8,128)S(1)}, f32[2,4,256,256]{3,2,1,0:T(8,128)}, u32[]{:S(2)}) copy-start(f32[2,4,256,256]{3,2,1,0:T(8,128)} %cross_ref.3) | copy-start | bytes 6291460
  113.3 1.6 copy-start.1
  118.7 31.0 %copy-start.8 = (f32[2,8,256]{2,1,0:T(8,128)S(1)}, f32[2,8,256]{2,1,0:T(8,128)}, u32[]{:S(2)}) copy-start(f32[2,8,256]{2,1,0:T(8,128)} %solution_ref.1) | copy-start | bytes 49156
  146.5 3.2 %collective-permute-start.6 = (f32[64,5,8,128]{3,2,1,0:T(8,128)S(1)}, f32[64,5,8,128]{3,2,1,0:T(8,128)}, u32[]{:S(2)}, u32[]{:S(2)}) collective-permute-start(f32[64,5,8,128]{3,2,1,0:T(8,128)S(1)} %all_to_all.15.mine_ref), channel_id=1, source_target_pairs={{0,1},{1,0},{2,3},{3,2},{4,5},{5,4},{6,7},{7,6},{8,9},{9,8},{10,11... | collective-permute-start | bytes 3932168 | tf_op jit(solution)/shard_map/ppermute | solution.py:390
  149.7 1.0 copy-start.3
  158.7 3.1 %collective-permute-start.7 = (f32[64,5,8,128]{3,2,1,0:T(8,128)S(1)}, f32[64,5,8,128]{3,2,1,0:T(8,128)S(1)}, u32[]{:S(2)}, u32[]{:S(2)}) collective-permute-start(f32[64,5,8,128]{3,2,1,0:T(8,128)S(1)} %slice.19), channel_id=1, source_target_pairs={{0,1},{1,0},{2,3},{3,2},{4,5},{5,4},{6,7},{7,6},{8,9},{9,8},{10,11... | collective-permute-start | bytes 3932168 | tf_op jit(solution)/shard_map/ppermute | solution.py:390
Sparse Core Ops, SparseCore 0:
  11.1 71.2 all-gather.1
where the time goes:
time: 197 us; the launch traced here: 196 us
  Pallas kernels  85.8 us (44%)
  blocking collectives  54.4 us (28%)
  waiting for transfers between devices  20.4 us (10%)
  starting transfers between devices  14.5 us (7%)
  between operations  14.3 us (7%)
  local copies, waits for them, and re-layouts  6.55 us (3%)
    pallas_call x3, Pallas kernels, add_image(): pl.pallas_call(functools.partial(image_kernel, pieces), grid=(pieces * ea...  68.3 us
    all_to_all x2, blocking collectives, exchange(): lax.all_to_all(value, AXES, 0, 0, axis_index_groups=groups, tiled=True)  54.4 us
    all_to_all x1, waiting for transfers between devices, exchange(): lax.all_to_all(value, AXES, 0, 0, axis_index_groups=groups, tiled=True)  13.6 us
    all_to_all x1, starting transfers between devices, exchange(): lax.all_to_all(value, AXES, 0, 0, axis_index_groups=groups, tiled=True)  8.41 us
    pallas_call x1, Pallas kernels, spread_step(): pl.pallas_call(spread_kernel, out_shape=(own, own, own, jax.ShapeDtypeStr...  7.89 us
    ppermute x5, waiting for transfers between devices, to_other_core(): return lax.ppermute(value, 'col', [(i, i ^ 1) for i in range(32)])  6.03 us
    ppermute x3, starting transfers between devices, per_device(): beyond = [x_around(hop)(same) for hop in (1, 3, 2)]  5.13 us
    pallas_call x1, Pallas kernels, point_payload(): pl.pallas_call(pick_points, out_shape=jax.ShapeDtypeStruct((copies, 6, RH...  4.97 us
  transfers between devices with their start and end apart: 10, of which 3 were waited for; matrix products, arithmetic and copies ran while one was open for 1% of the time, Pallas kernels for 37%

commit v1 on v0

--- a/solution.py
+++ b/solution.py
@@ -10,10 +10,9 @@
 
 f32 = jnp.float32
 bf16 = jnp.bfloat16
-highest = lax.Precision.HIGHEST
 rate = math.sqrt(3.0) / 0.3 * math.log2(math.e)
 offset = 1.0 / math.log(2.0)
-variance = 0.05 * math.log(2.0)
+variance = -0.05 * math.e * math.log(2.0)
 nugget = 1.0
 AXES = ("row", "col")
 BS, RHS, NBR, OWN = 256, 8, 4, 2
@@ -23,10 +22,6 @@
 MEGA = 1 << 20
 
 
-def dot(a, b, dims):
-    return lax.dot_general(a, b, (dims, ((), ())), precision=highest, preferred_element_type=f32)
-
-
 def split2(v):
     top = v.astype(bf16)
     return top, (v - top.astype(f32)).astype(bf16)
@@ -37,6 +32,13 @@
     rest = v - top
     middle = rest.astype(bf16).astype(f32)
     return top, middle, rest - middle
+
+
+def pair_dot(a, top, low, dims):
+    both = jnp.concatenate(split2(a), axis=0)
+    high = lax.dot_general(both, top, (dims, ((), ())), preferred_element_type=f32)
+    rest = lax.dot_general(both, low, (dims, ((), ())), preferred_element_type=f32)
+    return high[:RHS] + (high[RHS:] + (rest[:RHS] + rest[RHS:]))
 
 
 def features(place, own):
@@ -147,8 +149,8 @@
                     job % 2, part * BS : (part + 1) * BS, lanes * HALF : (lanes + 1) * HALF
                 ]
                 x = jnp.maximum(x, 1e-30)
-                t = x * lax.rsqrt(x)
-                tile = (t + offset) * jnp.exp2(-t)
+                u = -offset - x * lax.rsqrt(x)
+                tile = u * jnp.exp2(u)
                 top, low = split2(tile)
                 field = field_part[q * (TALL // BS) + part]
                 where = slice(r * WIDE + lanes * HALF, r * WIDE + (lanes + 1) * HALF)
@@ -192,18 +194,42 @@
     )(own, start, *columns)
 
 
-def lower(near, valid_ref, cross_ref, field, block):
+def split_kernel(cross_ref, whitening_ref, cross_top, cross_low, whiten_top, whiten_low):
+    def one(at, carry):
+        cross_top[at], cross_low[at] = split2(cross_ref[at])
+        return carry
+
+    lax.fori_loop(0, OWN * NBR, one, 0)
+    rows = lax.broadcasted_iota(jnp.int32, (BS, BS), 0)
+    lanes = lax.broadcasted_iota(jnp.int32, (BS, BS), 1)
+    for b in range(OWN):
+        whiten = whitening_ref[b] + jnp.where(rows == lanes, 1.0, 0.0)
+        whiten_top[b], whiten_low[b] = split2(whiten)
+
+
+def split_factors(cross, whitening):
+    vmem = pl.BlockSpec(memory_space=pltpu.VMEM)
+    shapes = [(OWN * NBR, BS, BS)] * 2 + [(OWN, BS, BS)] * 2
+    return pl.pallas_call(
+        split_kernel,
+        out_shape=tuple(jax.ShapeDtypeStruct(shape, bf16) for shape in shapes),
+        in_specs=[vmem] * 2,
+        out_specs=(vmem,) * 4,
+        compiler_params=pltpu.CompilerParams(vmem_limit_bytes=12 * MEGA),
+        cost_estimate=pl.CostEstimate(flops=4 << 20, transcendentals=0, bytes_accessed=5 << 20),
+        name="split_factors",
+    )(cross.reshape(OWN * NBR, BS, BS), whitening)
+
+
+def lower(near, valid_ref, cross_top, cross_low, field, block):
     total = field
     for k in range(NBR):
-        weight = valid_ref[block * NBR + k].astype(f32)
-        total = total - dot(near(block, k) * weight, cross_ref[block, k], ((1,), (1,)))
+        at = block * NBR + k
+        weight = valid_ref[at].astype(f32)
+        total = total - pair_dot(
+            near(at) * weight, cross_top[at], cross_low[at], ((1,), (1,))
+        )
     return total
-
-
-def whiten_of(whitening_ref, block):
-    rows = lax.broadcasted_iota(jnp.int32, (BS, BS), 0)
-    lanes = lax.broadcasted_iota(jnp.int32, (BS, BS), 1)
-    return whitening_ref[block] + jnp.where(rows == lanes, 1.0, 0.0)
 
 
 def lanes_of(v):
@@ -211,7 +237,8 @@
 
 
 def measure_kernel(
-    list_ref, valid_ref, all_ref, residual_ref, cross_ref, whitening_ref, sum_ref, direction_ref,
+    list_ref, valid_ref, all_ref, residual_ref, cross_top, cross_low, whiten_top, whiten_low,
+    sum_ref, direction_ref,
     out_ref, near_ref, near_buf, sems,
 ):
     copies = []
@@ -229,9 +256,9 @@
     tiles = []
     for b in range(OWN):
         lowered = lower(
-            lambda b, k: near_buf[b * NBR + k], valid_ref, cross_ref, residual_ref[b], b
-        )
-        mapped = dot(lowered, whiten_of(whitening_ref, b), ((1,), (1,)))
+            lambda at: near_buf[at], valid_ref, cross_top, cross_low, residual_ref[b], b
+        )
+        mapped = pair_dot(lowered, whiten_top[b], whiten_low[b], ((1,), (1,)))
         old = old + lanes_of(mapped * mapped)
         here = slice(b * BS, (b + 1) * BS)
         image = sum_ref[:RHS, here] + sum_ref[RHS:, here] + nugget * direction_ref[b]
@@ -251,7 +278,7 @@
     near_ref[...] = near_buf[...]
 
 
-def measure_step(lists, valid, gathered, residual, cross, whitening, total, direction):
+def measure_step(lists, valid, gathered, residual, factors, total, direction):
     smem = pl.BlockSpec(memory_space=pltpu.SMEM)
     vmem = pl.BlockSpec(memory_space=pltpu.VMEM)
     return pl.pallas_call(
@@ -260,7 +287,7 @@
             jax.ShapeDtypeStruct((PEERS, 5, RHS, HALF), f32),
             jax.ShapeDtypeStruct((OWN * NBR, RHS, BS), f32),
         ),
-        in_specs=[smem, smem, pl.BlockSpec(memory_space=pl.ANY), vmem, vmem, vmem, vmem, vmem],
+        in_specs=[smem, smem, pl.BlockSpec(memory_space=pl.ANY)] + [vmem] * 7,
         out_specs=(vmem, vmem),
         scratch_shapes=[
             pltpu.VMEM((OWN * NBR, RHS, BS), f32),
@@ -268,12 +295,12 @@
         ],
         compiler_params=pltpu.CompilerParams(vmem_limit_bytes=24 * MEGA),
         name="measure_step",
-    )(lists, valid, gathered, residual, cross, whitening, total, direction)
+    )(lists, valid, gathered, residual, *factors, total, direction)
 
 
 def spread_kernel(
     at_ref, valid_ref, into_ref, self_ref, mine_ref, other_ref, near_ref, residual_ref, solution_ref,
-    direction_ref, cross_ref, whitening_ref,
+    direction_ref, cross_top, cross_low, whiten_top, whiten_low,
     solution_out, residual_out, scaled_out, out_ref, old_out,
 ):
     total = jnp.zeros((RHS, HALF), f32)
@@ -304,17 +331,17 @@
         following = residual_ref[b] - step * image
         residual_out[b] = following
         lowered = lower(
-            lambda b, k: near_ref[b * NBR + k] - step * image_of(at_ref[b * NBR + k]),
-            valid_ref, cross_ref, following, b,
-        )
-        whiten = whiten_of(whitening_ref, b)
-        mapped = dot(lowered, whiten, ((1,), (1,)))
+            lambda at: near_ref[at] - step * image_of(at_ref[at]),
+            valid_ref, cross_top, cross_low, following, b,
+        )
+        mapped = pair_dot(lowered, whiten_top[b], whiten_low[b], ((1,), (1,)))
         newer = newer + lanes_of(mapped * mapped)
-        scaled = dot(mapped, whiten, ((1,), (0,)))
+        scaled = pair_dot(mapped, whiten_top[b], whiten_low[b], ((1,), (0,)))
         scaled_out[b] = scaled
         for k in range(NBR):
             at = b * NBR + k
-            spread = dot(scaled, cross_ref[b, k], ((1,), (0,))) * valid_ref[at].astype(f32)
+            spread = pair_dot(scaled, cross_top[at], cross_low[at], ((1,), (0,)))
+            spread = spread * valid_ref[at].astype(f32)
             to = into_ref[at]
             out_ref[to >> 1, 2 * (to & 1)] += spread[:, :HALF]
             out_ref[to >> 1, 2 * (to & 1) + 1] += spread[:, HALF:]
@@ -353,7 +380,7 @@
 
 
 def spread_step(
-    at, valid, into, self_at, mine, other, near, residual, solution, direction, cross, whitening
+    at, valid, into, self_at, mine, other, near, residual, solution, direction, factors
 ):
     smem = pl.BlockSpec(memory_space=pltpu.SMEM)
     vmem = pl.BlockSpec(memory_space=pltpu.VMEM)
@@ -367,13 +394,12 @@
             jax.ShapeDtypeStruct((2 * PEERS, 2 * OWN + 1, RHS, HALF), f32),
             jax.ShapeDtypeStruct((RHS, HALF), f32),
         ),
-        in_specs=[smem] * 4 + [vmem] * 8,
+        in_specs=[smem] * 4 + [vmem] * 10,
         out_specs=(vmem,) * 5,
         compiler_params=pltpu.CompilerParams(vmem_limit_bytes=40 * MEGA),
         name="spread_step",
     )(
-        at, valid, into, self_at, mine, other, near, residual, solution, direction, cross,
-        whitening,
+        at, valid, into, self_at, mine, other, near, residual, solution, direction, *factors
     )
 
 
@@ -395,9 +421,10 @@
 
 
 SAME_CORE = [[2 * j + core for j in range(PEERS)] for core in range(2)]
-SAME_X = [
-    [y * 32 + x * 8 + z * 2 + core for core in range(2) for y in range(4) for z in range(4)]
+SAME_X_CORE = [
+    [y * 32 + x * 8 + z * 2 + core for y in range(4) for z in range(4)]
     for x in range(4)
+    for core in range(2)
 ]
 
 
@@ -419,25 +446,22 @@
     gathered = lax.all_gather(residual, AXES, axis=0, tiled=True)
 
     own_order = lax.dynamic_slice_in_dim(ordering, device * (OWN * BS), OWN * BS, 0)
-    payload = point_payload(own_order, coordinates, direction, 32)
+    factors = split_factors(cross, whitening)
+    payload = point_payload(own_order, coordinates, direction, 16)
     own = payload[0]
-    plane = exchange(payload, SAME_X)
-    half = plane.shape[0] // 2
-    same = jnp.where(here_core == 0, plane[:half], plane[half:])
-    beyond = [x_around(hop)(same) for hop in (1, 3, 2)]
-    total = add_image(own, [plane], jnp.zeros((2 * RHS, OWN * BS), f32))
+    plane = exchange(payload, SAME_X_CORE)
+    plane, plane_other = lax.optimization_barrier((plane, to_other_core(plane)))
+    beyond = [x_around(hop)(plane) for hop in (1, 3, 2)]
+    total = add_image(own, [plane, plane_other], jnp.zeros((2 * RHS, OWN * BS), f32))
     others = [to_other_core(piece) for piece in beyond]
     total = add_image(own, beyond, total)
     total = add_image(own, others, total)
 
-    image, near = measure_step(
-        lists, valid, gathered, residual, cross, whitening, total, direction
-    )
+    image, near = measure_step(lists, valid, gathered, residual, factors, total, direction)
     mine = exchange(image, SAME_CORE)
     other = to_other_core(mine)
     solution_next, residual_next, scaled, back, old = spread_step(
-        at, valid, into, self_at, mine, other, near, residual, solution, direction, cross,
-        whitening,
+        at, valid, into, self_at, mine, other, near, residual, solution, direction, factors
     )
     back = back[:PEERS] + to_other_core(back[PEERS:])
     direction_next = sum_step(exchange(back, SAME_CORE), scaled, direction, old)

time: 197 us -> 192 us (0.975)
  Pallas kernels: 85.8 us -> 82.1 us
  waiting for transfers between devices: 20.4 us -> 16.7 us
  local copies, waits for them, and re-layouts: 6.55 us -> 9.05 us
    all_to_all x1, waiting for transfers between devices: 13.6 us -> 9.95 us  [exchange(): lax.all_to_all(value, AXES, 0, 0, axis_index_groups=groups, tiled=True)]
    pallas_call x1, Pallas kernels: 7.89 us -> 5.27 us  [spread_step(): pl.pallas_call(spread_kernel, out_shape=(own, own, own, jax.ShapeDtypeStr...]
    unnamed x20 -> x26, local copies, waits for them, and re-layouts: 4.6 us -> 7.05 us
    ppermute x5 -> x6, waiting for transfers between devices: 6.03 us -> 6.03 us  [to_other_core(): return lax.ppermute(value, 'col', [(i, i ^ 1) for i in range(32)])]
  transfers between devices with their start and end apart: 10 -> 11, of which waited for: 3 -> 3; matrix products, arithmetic and copies ran while one was open for 1% -> 1% of each run, Pallas kernels for 37% -> 39%
where the time goes in v1:
time: 192 us; the launch traced here: 191 us
  Pallas kernels  82.1 us (43%)
  blocking collectives  54.8 us (29%)
  waiting for transfers between devices  16.7 us (9%)
  between operations  14.3 us (7%)
  starting transfers between devices  14.2 us (7%)
  local copies, waits for them, and re-layouts  9.05 us (5%)
    pallas_call x3, Pallas kernels, add_image(): pl.pallas_call(functools.partial(image_kernel, pieces), grid=(pieces * ea...  68.9 us
    all_to_all x2, blocking collectives, exchange(): lax.all_to_all(value, AXES, 0, 0, axis_index_groups=groups, tiled=True)  54.8 us
    all_to_all x1, waiting for transfers between devices, exchange(): lax.all_to_all(value, AXES, 0, 0, axis_index_groups=groups, tiled=True)  9.95 us
    all_to_all x1, starting transfers between devices, exchange(): lax.all_to_all(value, AXES, 0, 0, axis_index_groups=groups, tiled=True)  8.18 us
    unnamed x26, local copies, waits for them, and re-layouts  7.05 us
    ppermute x6, waiting for transfers between devices, to_other_core(): return lax.ppermute(value, 'col', [(i, i ^ 1) for i in range(32)])  6.03 us
    pallas_call x1, Pallas kernels, spread_step(): pl.pallas_call(spread_kernel, out_shape=(own, own, own, jax.ShapeDtypeStr...  5.27 us
    ppermute x3, starting transfers between devices, per_device(): beyond = [x_around(hop)(plane) for hop in (1, 3, 2)]  5.06 us
  transfers between devices with their start and end apart: 11, of which 3 were waited for; matrix products, arithmetic and copies ran while one was open for 1% of the time, Pallas kernels for 39%

profile of v1, /device:TPU:0, one launch (start us, length us, event | category | flops | bytes accessed | tf_op | source)
XLA Modules:
  0.0 191.4 jit_solution(3705608231549253129)
XLA Ops:
  7.9 0.8 dynamic_slice.7.order_ref
  8.7 1.2 copy-done.2
  9.9 0.7 copy-done.8
  10.6 4.8 %pick_points.1 = f32[16,6,8,128]{3,2,1,0:T(8,128)} custom-call(s32[512]{0:T(512)S(1)} %dynamic_slice.7.order_ref, f32[3,65536]{1,0:T(4,128)S(1)} %copy-done.2, f32[2,8,256]{2,1,0:T(8,128)S(1)} %copy-done.8), custom_call_target="tpu_custom_call" | custom-call | tf_op jit(solution)/shard_map/pick_points/pallas_call | solution.py:92
  15.4 8.2 %all-to-all-start = ((f32[16,6,8,128]{3,2,1,0:T(8,128)}), f32[16,6,8,128]{3,2,1,0:T(8,128)}, u32[]{:S(2)}, u32[]{:S(2)}) async-start(f32[16,6,8,128]{3,2,1,0:T(8,128)} %pick_points.1), calls=%async_computation | async-start | bytes 786432 | tf_op jit(solution)/shard_map/all_to_all | solution.py:420
  23.6 9.9 %all-to-all-done.refs_0_ = f32[16,6,8,128]{3,2,1,0:T(8,128)} async-done(((f32[16,6,8,128]{3,2,1,0:T(8,128)}), f32[16,6,8,128]{3,2,1,0:T(8,128)}, u32[]{:S(2)}, u32[]{:S(2)}) %all-to-all-start) | async-done | bytes 393248 | tf_op jit(solution)/shard_map/all_to_all | solution.py:420
  34.0 1.6 copy-done
  36.0 0.8 slice_bitcast_fusion.own_ref
  36.8 3.0 %collective-permute-start.3 = (f32[16,6,8,128]{3,2,1,0:T(8,128)}, f32[16,6,8,128]{3,2,1,0:T(8,128)S(1)}, u32[]{:S(2)}, u32[]{:S(2)}) collective-permute-start(f32[16,6,8,128]{3,2,1,0:T(8,128)} %all-to-all-done.refs_0_), channel_id=1, source_target_pairs={{0,16},{1,17},{2,18},{3,19},{4,20},{5,21},{6,22},{7,23},{8,24},{9,... | collective-permute-start | bytes 1179656 | tf_op jit(solution)/shard_map/ppermute | solution.py:454
  39.8 1.1 collective-permute-start.2
  41.0 0.9 collective-permute-start.1
  41.9 18.0 %image.3.start_ref = f32[16,512]{1,0:T(8,128)S(1)} custom-call(f32[6,8,128]{2,1,0:T(8,128)S(1)} %slice_bitcast_fusion.own_ref, f32[16,512]{1,0:T(8,128)S(1)} %broadcast_in_dim.8.start_ref, f32[16,6,8,128]{3,2,1,0:T(8,128)} %all-to-all-done.refs_0_, f32[16,6,8,128]{3,2,1,0:T(8,128)} %collective-permute-done.refs_1_), custom_call_target="tpu_custom_call" | custom-call | flops 5033164800 | bytes 786432 | tf_op jit(solution)/shard_map/image/pallas_call | solution.py:173
  60.6 25.5 %image.4.start_ref = f32[16,512]{1,0:T(8,128)S(1)} custom-call(f32[6,8,128]{2,1,0:T(8,128)S(1)} %slice_bitcast_fusion.own_ref, f32[16,512]{1,0:T(8,128)S(1)} %image.3.start_ref, f32[16,6,8,128]{3,2,1,0:T(8,128)S(1)} %collective-permute-done.1.refs_0_, f32[16,6,8,128]{3,2,1,0:T(8,128)S(1)} %collective-permute-done.2.refs_1_, ...), custom_call_target="tpu_custom_call" | custom-call | flops 7549747200 | bytes 1179648 | tf_op jit(solution)/shard_map/image/pallas_call | solution.py:173
  86.1 25.4 %image.5.sum_ref = f32[16,512]{1,0:T(8,128)S(1)} custom-call(f32[6,8,128]{2,1,0:T(8,128)S(1)} %slice_bitcast_fusion.own_ref, f32[16,512]{1,0:T(8,128)S(1)} %image.4.start_ref, f32[16,6,8,128]{3,2,1,0:T(8,128)S(1)} %collective-permute-done.4.refs_0_, f32[16,6,8,128]{3,2,1,0:T(8,128)S(1)} %collective-permute-done.5.refs_1_, ...), custom_call_target="tpu_custom_call" | custom-call | flops 7549747200 | bytes 1179648 | tf_op jit(solution)/shard_map/image/pallas_call | solution.py:173
  111.6 1.6 copy-done.1
  113.2 2.0 %measure_step.1 = (f32[64,5,8,128]{3,2,1,0:T(8,128)S(1)}, f32[8,8,256]{2,1,0:T(8,128)S(1)}) custom-call(s32[8]{0:T(128)S(1)} %reshape.21.list_ref, s32[8]{0:T(128)S(1)} %reshape.26.valid_ref, f32[256,8,256]{2,1,0:T(8,128)S(1)} %copy-done.1, f32[2,8,256]{2,1,0:T(8,128)S(1)} %copy-done.10, bf16[8,256,256]{2,1,0:T(8,128)(2,1)S(1)} %get-tuple-element.16.cross_top, ...), custom_call_target="tpu_custom_call" | custom-call | tf_op jit(solution)/shard_map/measure_step/pallas_call | solution.py:284
  115.3 28.2 %all_to_all.15.mine_ref = f32[64,5,8,128]{3,2,1,0:T(8,128)S(1)} all-to-all(f32[64,5,8,128]{3,2,1,0:T(8,128)S(1)} %get-tuple-element.22), channel_id=1, replica_groups={{0,2,4,6,8,10,12,14,16,18,20,22,24,26,28,30,32,34,36,38,40,42,44,46,48,..., dimensions={0} | all-to-all | bytes 2621440 | tf_op jit(solution)/shard_map/all_to_all | solution.py:420
  143.5 3.1 %collective-permute-done.7.other_ref = f32[64,5,8,128]{3,2,1,0:T(8,128)} collective-permute-done((f32[64,5,8,128]{3,2,1,0:T(8,128)S(1)}, f32[64,5,8,128]{3,2,1,0:T(8,128)}, u32[]{:S(2)}, u32[]{:S(2)}) %collective-permute-start.7) | collective-permute-done | bytes 1310752 | tf_op jit(solution)/shard_map/ppermute | solution.py:416
  146.7 0.9 copy-done.4
  147.6 0.9 copy-done.6
  148.6 5.3 %spread_step.1 = (f32[2,8,256]{2,1,0:T(8,128)}, f32[2,8,256]{2,1,0:T(8,128)}, f32[2,8,256]{2,1,0:T(8,128)S(1)}, f32[128,5,8,128]{3,2,1,0:T(8,128)S(1)}, f32[8,128]{1,0:T(8,128)S(1)}) custom-call(s32[8]{0:T(128)S(1)} %multiply_add_fusion.1.at_ref, s32[8]{0:T(128)S(1)} %reshape.26.valid_ref, s32[8]{0:T(128)S(1)} %get-tuple-element.29.into_ref, ...), custom_call_target="tpu_custom_call" | custom-call | tf_op jit(solution)/shard_map/spread_step/pallas_call | solution.py:388
  154.1 2.9 %collective-permute-done.8 = f32[64,5,8,128]{3,2,1,0:T(8,128)S(1)} collective-permute-done((f32[64,5,8,128]{3,2,1,0:T(8,128)S(1)}, f32[64,5,8,128]{3,2,1,0:T(8,128)S(1)}, u32[]{:S(2)}, u32[]{:S(2)}) %collective-permute-start.8) | collective-permute-done | bytes 1310752 | tf_op jit(solution)/shard_map/ppermute | solution.py:416
  157.2 26.6 %all_to_all.16.all_ref = f32[64,5,8,128]{3,2,1,0:T(8,128)S(1)} all-to-all(f32[64,5,8,128]{3,2,1,0:T(8,128)S(1)} %slice_add_fusion), channel_id=1, replica_groups={{0,2,4,6,8,10,12,14,16,18,20,22,24,26,28,30,32,34,36,38,40,42,44,46,48,..., dimensions={0} | all-to-all | bytes 2621440 | tf_op jit(solution)/shard_map/all_to_all | solution.py:420
  183.8 0.7 sum_step.1
  (49 shorter events, 2.8 us)
Async XLA Ops:
  7.2 26.4 %copy-start.12 = (s32[256,4]{0,1:T(4,128)S(1)}, s32[256,4]{0,1:T(4,128)}, u32[]{:S(2)}) copy-start(s32[256,4]{0,1:T(4,128)} %param.10) | copy-start | bytes 12292
  7.2 104.4 %all-gather.2.cloned.1.call-start = ((), (), s32[]{:S(2)}) async-start(), calls=%async_computation.3 | async-start | bytes 2113536 | tf_op jit(solution)/shard_map/all_gather | solution.py:446
  8.7 1.2 copy-start.2
  9.9 0.7 copy-start.8
  10.6 23.3 %copy-start.7 = (f32[2,256,256]{2,1,0:T(8,128)S(1)}, f32[2,256,256]{2,1,0:T(8,128)}, u32[]{:S(2)}) copy-start(f32[2,256,256]{2,1,0:T(8,128)} %whitening_ref.1) | copy-start | bytes 1572868
  15.4 18.1 %all-to-all-start = ((f32[16,6,8,128]{3,2,1,0:T(8,128)}), f32[16,6,8,128]{3,2,1,0:T(8,128)}, u32[]{:S(2)}, u32[]{:S(2)}) async-start(f32[16,6,8,128]{3,2,1,0:T(8,128)} %pick_points.1), calls=%async_computation | async-start | bytes 786432 | tf_op jit(solution)/shard_map/all_to_all | solution.py:420
  33.5 3.3 %collective-permute-start = (f32[16,6,8,128]{3,2,1,0:T(8,128)}, f32[16,6,8,128]{3,2,1,0:T(8,128)}, u32[]{:S(2)}, u32[]{:S(2)}) collective-permute-start(f32[16,6,8,128]{3,2,1,0:T(8,128)} %all-to-all-done.refs_0_), channel_id=1, source_target_pairs={{0,1},{1,0},{2,3},{3,2},{4,5},{5,4},{6,7},{7,6},{8,9},{9,8},{10,11... | collective-permute-start | bytes 1179656 | tf_op jit(solution)/shard_map/ppermute | solution.py:416
  34.0 1.6 copy-start
  36.0 75.6 %copy-start.3 = (bf16[2,256,256]{2,1,0:T(8,128)(2,1)}, bf16[2,256,256]{2,1,0:T(8,128)(2,1)S(1)}, u32[]{:S(2)}) copy-start(bf16[2,256,256]{2,1,0:T(8,128)(2,1)S(1)} %get-tuple-element.18.whiten_top) | copy-start | bytes 786436
  36.0 75.6 %copy-start.5 = (bf16[2,256,256]{2,1,0:T(8,128)(2,1)}, bf16[2,256,256]{2,1,0:T(8,128)(2,1)S(1)}, u32[]{:S(2)}) copy-start(bf16[2,256,256]{2,1,0:T(8,128)(2,1)S(1)} %get-tuple-element.19.whiten_low) | copy-start | bytes 786436
  36.8 23.1 %collective-permute-start.3 = (f32[16,6,8,128]{3,2,1,0:T(8,128)}, f32[16,6,8,128]{3,2,1,0:T(8,128)S(1)}, u32[]{:S(2)}, u32[]{:S(2)}) collective-permute-start(f32[16,6,8,128]{3,2,1,0:T(8,128)} %all-to-all-done.refs_0_), channel_id=1, source_target_pairs={{0,16},{1,17},{2,18},{3,19},{4,20},{5,21},{6,22},{7,23},{8,24},{9,... | collective-permute-start | bytes 1179656 | tf_op jit(solution)/shard_map/ppermute | solution.py:454
  39.8 20.1 %collective-permute-start.2 = (f32[16,6,8,128]{3,2,1,0:T(8,128)}, f32[16,6,8,128]{3,2,1,0:T(8,128)S(1)}, u32[]{:S(2)}, u32[]{:S(2)}) collective-permute-start(f32[16,6,8,128]{3,2,1,0:T(8,128)} %all-to-all-done.refs_0_), channel_id=1, source_target_pairs={{0,24},{1,25},{2,26},{3,27},{4,28},{5,29},{6,30},{7,31},{8,0},{9,1... | collective-permute-start | bytes 1179656 | tf_op jit(solution)/shard_map/ppermute | solution.py:454
  41.0 19.5 %collective-permute-start.1 = (f32[16,6,8,128]{3,2,1,0:T(8,128)}, f32[16,6,8,128]{3,2,1,0:T(8,128)S(1)}, u32[]{:S(2)}, u32[]{:S(2)}) collective-permute-start(f32[16,6,8,128]{3,2,1,0:T(8,128)} %all-to-all-done.refs_0_), channel_id=1, source_target_pairs={{0,8},{1,9},{2,10},{3,11},{4,12},{5,13},{6,14},{7,15},{8,16},{9,17... | collective-permute-start | bytes 1179656 | tf_op jit(solution)/shard_map/ppermute | solution.py:454
  59.9 26.2 %collective-permute-start.6 = (f32[16,6,8,128]{3,2,1,0:T(8,128)S(1)}, f32[16,6,8,128]{3,2,1,0:T(8,128)S(1)}, u32[]{:S(2)}, u32[]{:S(2)}) collective-permute-start(f32[16,6,8,128]{3,2,1,0:T(8,128)S(1)} %collective-permute-done.3.refs_2_), channel_id=1, source_target_pairs={{0,1},{1,0},{2,3},{3,2},{4,5},{5,4},{6,7},{7,6},{8,9},{9,8},{10,11... | collective-permute-start | bytes 1179656 | tf_op jit(solution)/shard_map/ppermute | solution.py:416
  60.0 26.1 %collective-permute-start.5 = (f32[16,6,8,128]{3,2,1,0:T(8,128)S(1)}, f32[16,6,8,128]{3,2,1,0:T(8,128)S(1)}, u32[]{:S(2)}, u32[]{:S(2)}) collective-permute-start(f32[16,6,8,128]{3,2,1,0:T(8,128)S(1)} %collective-permute-done.2.refs_1_), channel_id=1, source_target_pairs={{0,1},{1,0},{2,3},{3,2},{4,5},{5,4},{6,7},{7,6},{8,9},{9,8},{10,11... | collective-permute-start | bytes 1179656 | tf_op jit(solution)/shard_map/ppermute | solution.py:416
  60.5 25.6 %collective-permute-start.4 = (f32[16,6,8,128]{3,2,1,0:T(8,128)S(1)}, f32[16,6,8,128]{3,2,1,0:T(8,128)S(1)}, u32[]{:S(2)}, u32[]{:S(2)}) collective-permute-start(f32[16,6,8,128]{3,2,1,0:T(8,128)S(1)} %collective-permute-done.1.refs_0_), channel_id=1, source_target_pairs={{0,1},{1,0},{2,3},{3,2},{4,5},{5,4},{6,7},{7,6},{8,9},{9,8},{10,11... | collective-permute-start | bytes 1179656 | tf_op jit(solution)/shard_map/ppermute | solution.py:416
  86.0 25.5 %copy-start.9 = (f32[2,8,256]{2,1,0:T(8,128)S(1)}, f32[2,8,256]{2,1,0:T(8,128)}, u32[]{:S(2)}) copy-start(f32[2,8,256]{2,1,0:T(8,128)} %direction_ref.7) | copy-start | bytes 49156
  86.0 25.5 %copy-start.10 = (f32[2,8,256]{2,1,0:T(8,128)S(1)}, f32[2,8,256]{2,1,0:T(8,128)}, u32[]{:S(2)}) copy-start(f32[2,8,256]{2,1,0:T(8,128)} %residual_ref.3) | copy-start | bytes 49156
  111.6 1.6 copy-start.1
  115.2 31.4 %copy-start.11 = (f32[2,8,256]{2,1,0:T(8,128)S(1)}, f32[2,8,256]{2,1,0:T(8,128)}, u32[]{:S(2)}) copy-start(f32[2,8,256]{2,1,0:T(8,128)} %solution_ref.1) | copy-start | bytes 49156
  143.5 3.2 %collective-permute-start.7 = (f32[64,5,8,128]{3,2,1,0:T(8,128)S(1)}, f32[64,5,8,128]{3,2,1,0:T(8,128)}, u32[]{:S(2)}, u32[]{:S(2)}) collective-permute-start(f32[64,5,8,128]{3,2,1,0:T(8,128)S(1)} %all_to_all.15.mine_ref), channel_id=1, source_target_pairs={{0,1},{1,0},{2,3},{3,2},{4,5},{5,4},{6,7},{7,6},{8,9},{9,8},{10,11... | collective-permute-start | bytes 3932168 | tf_op jit(solution)/shard_map/ppermute | solution.py:416
  146.7 1.0 copy-start.4
  147.6 0.9 copy-start.6
  153.9 3.1 %collective-permute-start.8 = (f32[64,5,8,128]{3,2,1,0:T(8,128)S(1)}, f32[64,5,8,128]{3,2,1,0:T(8,128)S(1)}, u32[]{:S(2)}, u32[]{:S(2)}) collective-permute-start(f32[64,5,8,128]{3,2,1,0:T(8,128)S(1)} %slice.11), channel_id=1, source_target_pairs={{0,1},{1,0},{2,3},{3,2},{4,5},{5,4},{6,7},{7,6},{8,9},{9,8},{10,11... | collective-permute-start | bytes 3932168 | tf_op jit(solution)/shard_map/ppermute | solution.py:416
Sparse Core Ops, SparseCore 0:
  11.2 68.8 all-gather.1

commit v2 on v1

--- a/solution.py
+++ b/solution.py
@@ -19,6 +19,7 @@
 HALF = 128
 STEP = 4
 PEERS = 64
+PAIR = 2 * OWN * BS
 MEGA = 1 << 20
 
 
@@ -57,21 +58,32 @@
     return jnp.concatenate([tiles[4, rows, :], tiles[5, rows, :]], axis=1)
 
 
-def pick_points(order_ref, coordinates_ref, direction_ref, out_ref):
+def pick_points(
+    all_order, all_coordinates, direction_ref, out_ref, order_ref, coordinates_ref, sems
+):
+    device = lax.axis_index("row") * 32 + lax.axis_index("col")
+    pair = pl.multiple_of(device // 2 * PAIR, PAIR)
+    order_copy = pltpu.make_async_copy(all_order.at[pl.ds(pair, PAIR)], order_ref, sems.at[0])
+    order_copy.start()
+    copy_points = pltpu.make_async_copy(all_coordinates, coordinates_ref, sems.at[1])
+    copy_points.start()
+    order_copy.wait()
+    copy_points.wait()
+    first = device % 2 * (OWN * BS)
     lane = lax.broadcasted_iota(jnp.int32, (3, HALF), 1)
     groups = 2 * OWN
 
     def one_point(i, found):
         kept = []
         for group in range(groups):
-            at = order_ref[group * HALF + i]
+            at = order_ref[first + group * HALF + i]
             base = pl.multiple_of((at >> 7) << 7, HALF)
             line = coordinates_ref[:, pl.ds(base, HALF)]
             turned = pltpu.roll(line, (i - (at & (HALF - 1))) & (HALF - 1), 1)
             kept.append(jnp.where(lane == i, turned, found[group]))
         return tuple(kept)
 
-    found = lax.fori_loop(0, HALF, one_point, (jnp.zeros((3, HALF), f32),) * groups, unroll=4)
+    found = lax.fori_loop(0, HALF, one_point, (jnp.zeros((3, HALF), f32),) * groups, unroll=16)
     pad = jnp.zeros((2, HALF), f32)
     tiles = []
     for block in range(OWN):
@@ -88,19 +100,24 @@
     lax.fori_loop(0, out_ref.shape[0], copy, 0)
 
 
-def point_payload(own_order, coordinates, direction, copies):
+def point_payload(ordering, coordinates, direction, copies):
     return pl.pallas_call(
         pick_points,
         out_shape=jax.ShapeDtypeStruct((copies, 6, RHS, HALF), f32),
         in_specs=[
-            pl.BlockSpec(memory_space=pltpu.SMEM),
-            pl.BlockSpec(memory_space=pltpu.VMEM),
+            pl.BlockSpec(memory_space=pltpu.HBM),
+            pl.BlockSpec(memory_space=pltpu.HBM),
             pl.BlockSpec(memory_space=pltpu.VMEM),
         ],
         out_specs=pl.BlockSpec(memory_space=pltpu.VMEM),
-        compiler_params=pltpu.CompilerParams(vmem_limit_bytes=8 * MEGA),
+        scratch_shapes=[
+            pltpu.SMEM((PAIR,), jnp.int32),
+            pltpu.VMEM(coordinates.shape, f32),
+            pltpu.SemaphoreType.DMA((2,)),
+        ],
+        compiler_params=pltpu.CompilerParams(vmem_limit_bytes=56 * MEGA),
         name="pick_points",
-    )(own_order, coordinates, direction)
+    )(ordering, coordinates, direction)
 
 
 TALL, WIDE = 512, 256
@@ -186,7 +203,7 @@
             pltpu.VMEM((OWN * STEP, 2 * RHS, BS), bf16),
             pltpu.VMEM((2, TALL, WIDE), f32),
         ],
-        compiler_params=pltpu.CompilerParams(vmem_limit_bytes=24 * MEGA),
+        compiler_params=pltpu.CompilerParams(vmem_limit_bytes=10 * MEGA),
         cost_estimate=pl.CostEstimate(
             flops=600 * pairs, transcendentals=2 * pairs, bytes_accessed=pieces * count * 6 * 4096
         ),
@@ -194,12 +211,7 @@
     )(own, start, *columns)
 
 
-def split_kernel(cross_ref, whitening_ref, cross_top, cross_low, whiten_top, whiten_low):
-    def one(at, carry):
-        cross_top[at], cross_low[at] = split2(cross_ref[at])
-        return carry
-
-    lax.fori_loop(0, OWN * NBR, one, 0)
+def split_whitening(whitening_ref, whiten_top, whiten_low):
     rows = lax.broadcasted_iota(jnp.int32, (BS, BS), 0)
     lanes = lax.broadcasted_iota(jnp.int32, (BS, BS), 1)
     for b in range(OWN):
@@ -207,18 +219,25 @@
         whiten_top[b], whiten_low[b] = split2(whiten)
 
 
-def split_factors(cross, whitening):
+def split_kernel(cross_ref, cross_top, cross_low):
+    def one(at, carry):
+        cross_top[at], cross_low[at] = split2(cross_ref[at])
+        return carry
+
+    lax.fori_loop(0, OWN * NBR, one, 0)
+
+
+def split_factors(cross):
     vmem = pl.BlockSpec(memory_space=pltpu.VMEM)
-    shapes = [(OWN * NBR, BS, BS)] * 2 + [(OWN, BS, BS)] * 2
     return pl.pallas_call(
         split_kernel,
-        out_shape=tuple(jax.ShapeDtypeStruct(shape, bf16) for shape in shapes),
-        in_specs=[vmem] * 2,
-        out_specs=(vmem,) * 4,
+        out_shape=(jax.ShapeDtypeStruct((OWN * NBR, BS, BS), bf16),) * 2,
+        in_specs=[vmem],
+        out_specs=(vmem,) * 2,
         compiler_params=pltpu.CompilerParams(vmem_limit_bytes=12 * MEGA),
         cost_estimate=pl.CostEstimate(flops=4 << 20, transcendentals=0, bytes_accessed=5 << 20),
         name="split_factors",
-    )(cross.reshape(OWN * NBR, BS, BS), whitening)
+    )(cross.reshape(OWN * NBR, BS, BS))
 
 
 def lower(near, valid_ref, cross_top, cross_low, field, block):
@@ -237,9 +256,9 @@
 
 
 def measure_kernel(
-    list_ref, valid_ref, all_ref, residual_ref, cross_top, cross_low, whiten_top, whiten_low,
+    list_ref, valid_ref, all_ref, residual_ref, cross_top, cross_low, whitening_ref,
     sum_ref, direction_ref,
-    out_ref, near_ref, near_buf, sems,
+    out_ref, near_ref, near_buf, whiten_top, whiten_low, sems,
 ):
     copies = []
     for b in range(OWN):
@@ -249,6 +268,7 @@
                 pltpu.make_async_copy(all_ref.at[list_ref[at]], near_buf.at[at], sems.at[at])
             )
             copies[-1].start()
+    split_whitening(whitening_ref, whiten_top, whiten_low)
     for copy in copies:
         copy.wait()
     old = jnp.zeros((RHS, HALF), f32)
@@ -287,22 +307,26 @@
             jax.ShapeDtypeStruct((PEERS, 5, RHS, HALF), f32),
             jax.ShapeDtypeStruct((OWN * NBR, RHS, BS), f32),
         ),
-        in_specs=[smem, smem, pl.BlockSpec(memory_space=pl.ANY)] + [vmem] * 7,
+        in_specs=[smem, smem, pl.BlockSpec(memory_space=pl.ANY)] + [vmem] * 6,
         out_specs=(vmem, vmem),
         scratch_shapes=[
             pltpu.VMEM((OWN * NBR, RHS, BS), f32),
+            pltpu.VMEM((OWN, BS, BS), bf16),
+            pltpu.VMEM((OWN, BS, BS), bf16),
             pltpu.SemaphoreType.DMA((OWN * NBR,)),
         ],
-        compiler_params=pltpu.CompilerParams(vmem_limit_bytes=24 * MEGA),
+        compiler_params=pltpu.CompilerParams(vmem_limit_bytes=8 * MEGA),
         name="measure_step",
     )(lists, valid, gathered, residual, *factors, total, direction)
 
 
 def spread_kernel(
     at_ref, valid_ref, into_ref, self_ref, mine_ref, other_ref, near_ref, residual_ref, solution_ref,
-    direction_ref, cross_top, cross_low, whiten_top, whiten_low,
+    direction_ref, cross_top, cross_low, whitening_ref,
     solution_out, residual_out, scaled_out, out_ref, old_out,
+    whiten_top, whiten_low,
 ):
+    split_whitening(whitening_ref, whiten_top, whiten_low)
     total = jnp.zeros((RHS, HALF), f32)
     for i in range(PEERS):
         total = total + mine_ref[i, 4] + other_ref[i, 4]
@@ -394,9 +418,13 @@
             jax.ShapeDtypeStruct((2 * PEERS, 2 * OWN + 1, RHS, HALF), f32),
             jax.ShapeDtypeStruct((RHS, HALF), f32),
         ),
-        in_specs=[smem] * 4 + [vmem] * 10,
+        in_specs=[smem] * 4 + [vmem] * 9,
         out_specs=(vmem,) * 5,
-        compiler_params=pltpu.CompilerParams(vmem_limit_bytes=40 * MEGA),
+        scratch_shapes=[
+            pltpu.VMEM((OWN, BS, BS), bf16),
+            pltpu.VMEM((OWN, BS, BS), bf16),
+        ],
+        compiler_params=pltpu.CompilerParams(vmem_limit_bytes=16 * MEGA),
         name="spread_step",
     )(
         at, valid, into, self_at, mine, other, near, residual, solution, direction, *factors
@@ -445,9 +473,8 @@
 
     gathered = lax.all_gather(residual, AXES, axis=0, tiled=True)
 
-    own_order = lax.dynamic_slice_in_dim(ordering, device * (OWN * BS), OWN * BS, 0)
-    factors = split_factors(cross, whitening)
-    payload = point_payload(own_order, coordinates, direction, 16)
+    factors = (*split_factors(cross), whitening)
+    payload = point_payload(ordering, coordinates, direction, 16)
     own = payload[0]
     plane = exchange(payload, SAME_X_CORE)
     plane, plane_other = lax.optimization_barrier((plane, to_other_core(plane)))
@@ -455,6 +482,7 @@
     total = add_image(own, [plane, plane_other], jnp.zeros((2 * RHS, OWN * BS), f32))
     others = [to_other_core(piece) for piece in beyond]
     total = add_image(own, beyond, total)
+    total, gathered = lax.optimization_barrier((total, gathered))
     total = add_image(own, others, total)
 
     image, near = measure_step(lists, valid, gathered, residual, factors, total, direction)

time: 192 us -> 190 us (0.990)
  local copies, waits for them, and re-layouts: 9.05 us -> 5.61 us
    unnamed x26 -> x20, local copies, waits for them, and re-layouts: 7.05 us -> 4.42 us
  transfers between devices with their start and end apart: 11 -> 11, of which waited for: 3 -> 3; matrix products, arithmetic and copies ran while one was open for 1% -> 1% of each run, Pallas kernels for 39% -> 26%
where the time goes in v2:
time: 190 us; the launch traced here: 189 us
  Pallas kernels  83.7 us (44%)
  blocking collectives  54.9 us (29%)
  waiting for transfers between devices  16.5 us (9%)
  between operations  14.3 us (8%)
  starting transfers between devices  14.1 us (7%)
  local copies, waits for them, and re-layouts  5.61 us (3%)
    pallas_call x3, Pallas kernels, add_image(): pl.pallas_call(functools.partial(image_kernel, pieces), grid=(pieces * ea...  70.5 us
    all_to_all x2, blocking collectives, exchange(): lax.all_to_all(value, AXES, 0, 0, axis_index_groups=groups, tiled=True)  54.9 us
    all_to_all x1, waiting for transfers between devices, exchange(): lax.all_to_all(value, AXES, 0, 0, axis_index_groups=groups, tiled=True)  9.8 us
    all_to_all x1, starting transfers between devices, exchange(): lax.all_to_all(value, AXES, 0, 0, axis_index_groups=groups, tiled=True)  8.14 us
    ppermute x6, waiting for transfers between devices, to_other_core(): return lax.ppermute(value, 'col', [(i, i ^ 1) for i in range(32)])  6.03 us
    pallas_call x1, Pallas kernels, spread_step(): pl.pallas_call(spread_kernel, out_shape=(own, own, own, jax.ShapeDtypeStr...  5.35 us
    ppermute x3, starting transfers between devices, per_device(): beyond = [x_around(hop)(plane) for hop in (1, 3, 2)]  5.05 us
    pallas_call x1, Pallas kernels, point_payload(): pl.pallas_call(pick_points, out_shape=jax.ShapeDtypeStruct((copies, 6, RH...  4.7 us
  transfers between devices with their start and end apart: 11, of which 3 were waited for; matrix products, arithmetic and copies ran while one was open for 1% of the time, Pallas kernels for 26%

profile of v2, /device:TPU:0, one launch (start us, length us, event | category | flops | bytes accessed | tf_op | source)
XLA Modules:
  0.0 189.4 jit_solution(15951160347676627109)
XLA Ops:
  7.2 0.7 all-gather.2.cloned.1.call-update
  7.9 4.7 %pick_points.1 = f32[16,6,8,128]{3,2,1,0:T(8,128)} custom-call(s32[65536]{0:T(1024)} %all_order.1, f32[3,65536]{1,0:T(4,128)} %all_coordinates.1, f32[2,8,256]{2,1,0:T(8,128)} %direction_ref.7), custom_call_target="tpu_custom_call" | custom-call | tf_op jit(solution)/shard_map/pick_points/pallas_call | solution.py:104
  12.6 8.1 %all-to-all-start = ((f32[16,6,8,128]{3,2,1,0:T(8,128)}), f32[16,6,8,128]{3,2,1,0:T(8,128)S(1)}, u32[]{:S(2)}, u32[]{:S(2)}) async-start(f32[16,6,8,128]{3,2,1,0:T(8,128)} %pick_points.1), calls=%async_computation | async-start | bytes 786432 | tf_op jit(solution)/shard_map/all_to_all | solution.py:448
  20.8 9.8 %all-to-all-done.refs_0_ = f32[16,6,8,128]{3,2,1,0:T(8,128)S(1)} async-done(((f32[16,6,8,128]{3,2,1,0:T(8,128)}), f32[16,6,8,128]{3,2,1,0:T(8,128)S(1)}, u32[]{:S(2)}, u32[]{:S(2)}) %all-to-all-start) | async-done | bytes 393248 | tf_op jit(solution)/shard_map/all_to_all | solution.py:448
  31.0 1.6 copy-done
  32.6 0.3 split_factors.1
  32.9 0.7 slice_bitcast_fusion.own_ref
  33.7 0.8 copy-done.7
  34.4 3.0 %collective-permute-start.3 = (f32[16,6,8,128]{3,2,1,0:T(8,128)S(1)}, f32[16,6,8,128]{3,2,1,0:T(8,128)S(1)}, u32[]{:S(2)}, u32[]{:S(2)}) collective-permute-start(f32[16,6,8,128]{3,2,1,0:T(8,128)S(1)} %all-to-all-done.refs_0_), channel_id=1, source_target_pairs={{0,16},{1,17},{2,18},{3,19},{4,20},{5,21},{6,22},{7,23},{8,24},{9,... | collective-permute-start | bytes 1179656 | tf_op jit(solution)/shard_map/ppermute | solution.py:481
  37.5 1.1 collective-permute-start.2
  38.6 0.9 collective-permute-start.1
  39.5 1.0 copy-done.8
  40.5 16.9 %image.3.start_ref = f32[16,512]{1,0:T(8,128)S(1)} custom-call(f32[6,8,128]{2,1,0:T(8,128)S(1)} %slice_bitcast_fusion.own_ref, f32[16,512]{1,0:T(8,128)S(1)} %broadcast_in_dim.8.start_ref, f32[16,6,8,128]{3,2,1,0:T(8,128)S(1)} %all-to-all-done.refs_0_, f32[16,6,8,128]{3,2,1,0:T(8,128)S(1)} %copy-done.8), custom_call_target="tpu_custom_call" | custom-call | flops 5033164800 | bytes 786432 | tf_op jit(solution)/shard_map/image/pallas_call | solution.py:190
  57.5 0.5 collective-permute-start.5
  58.1 26.6 %image.4.start_ref = f32[16,512]{1,0:T(8,128)S(1)} custom-call(f32[6,8,128]{2,1,0:T(8,128)S(1)} %slice_bitcast_fusion.own_ref, f32[16,512]{1,0:T(8,128)S(1)} %image.3.start_ref, f32[16,6,8,128]{3,2,1,0:T(8,128)} %collective-permute-done.1.refs_0_, f32[16,6,8,128]{3,2,1,0:T(8,128)} %collective-permute-done.2.refs_1_, ...), custom_call_target="tpu_custom_call" | custom-call | flops 7549747200 | bytes 1179648 | tf_op jit(solution)/shard_map/image/pallas_call | solution.py:190
  84.8 27.0 %image.5.sum_ref = f32[16,512]{1,0:T(8,128)S(1)} custom-call(f32[6,8,128]{2,1,0:T(8,128)S(1)} %slice_bitcast_fusion.own_ref, f32[16,512]{1,0:T(8,128)S(1)} %image.4.start_ref, f32[16,6,8,128]{3,2,1,0:T(8,128)} %collective-permute-done.4.refs_0_, f32[16,6,8,128]{3,2,1,0:T(8,128)} %collective-permute-done.5.refs_1_, ...), custom_call_target="tpu_custom_call" | custom-call | flops 7549747200 | bytes 1179648 | tf_op jit(solution)/shard_map/image/pallas_call | solution.py:190
  111.9 2.1 %measure_step.1 = (f32[64,5,8,128]{3,2,1,0:T(8,128)S(1)}, f32[8,8,256]{2,1,0:T(8,128)S(1)}) custom-call(s32[8]{0:T(128)S(1)} %reshape.21.list_ref, s32[8]{0:T(128)S(1)} %reshape.26.valid_ref, f32[256,8,256]{2,1,0:T(8,128)S(1)} %copy-done.1, f32[2,8,256]{2,1,0:T(8,128)S(1)} %copy-done.5, bf16[8,256,256]{2,1,0:T(8,128)(2,1)S(1)} %get-tuple-element.19.cross_top, ...), custom_call_target="tpu_custom_call" | custom-call | tf_op jit(solution)/shard_map/measure_step/pallas_call | solution.py:304
  114.0 28.3 %all_to_all.15.mine_ref = f32[64,5,8,128]{3,2,1,0:T(8,128)S(1)} all-to-all(f32[64,5,8,128]{3,2,1,0:T(8,128)S(1)} %get-tuple-element.22), channel_id=1, replica_groups={{0,2,4,6,8,10,12,14,16,18,20,22,24,26,28,30,32,34,36,38,40,42,44,46,48,..., dimensions={0} | all-to-all | bytes 2621440 | tf_op jit(solution)/shard_map/all_to_all | solution.py:448
  142.3 3.1 %collective-permute-done.7.other_ref = f32[64,5,8,128]{3,2,1,0:T(8,128)} collective-permute-done((f32[64,5,8,128]{3,2,1,0:T(8,128)S(1)}, f32[64,5,8,128]{3,2,1,0:T(8,128)}, u32[]{:S(2)}, u32[]{:S(2)}) %collective-permute-start.7) | collective-permute-done | bytes 1310752 | tf_op jit(solution)/shard_map/ppermute | solution.py:444
  145.4 1.0 copy-done.3
  146.5 5.3 %spread_step.1 = (f32[2,8,256]{2,1,0:T(8,128)}, f32[2,8,256]{2,1,0:T(8,128)}, f32[2,8,256]{2,1,0:T(8,128)S(1)}, f32[128,5,8,128]{3,2,1,0:T(8,128)S(1)}, f32[8,128]{1,0:T(8,128)S(1)}) custom-call(s32[8]{0:T(128)S(1)} %multiply_add_fusion.1.at_ref, s32[8]{0:T(128)S(1)} %reshape.26.valid_ref, s32[8]{0:T(128)S(1)} %get-tuple-element.29.into_ref, ...), custom_call_target="tpu_custom_call" | custom-call | tf_op jit(solution)/shard_map/spread_step/pallas_call | solution.py:412
  152.1 2.9 %collective-permute-done.8 = f32[64,5,8,128]{3,2,1,0:T(8,128)S(1)} collective-permute-done((f32[64,5,8,128]{3,2,1,0:T(8,128)S(1)}, f32[64,5,8,128]{3,2,1,0:T(8,128)S(1)}, u32[]{:S(2)}, u32[]{:S(2)}) %collective-permute-start.8) | collective-permute-done | bytes 1310752 | tf_op jit(solution)/shard_map/ppermute | solution.py:444
  155.2 26.6 %all_to_all.16.all_ref = f32[64,5,8,128]{3,2,1,0:T(8,128)S(1)} all-to-all(f32[64,5,8,128]{3,2,1,0:T(8,128)S(1)} %slice_add_fusion), channel_id=1, replica_groups={{0,2,4,6,8,10,12,14,16,18,20,22,24,26,28,30,32,34,36,38,40,42,44,46,48,..., dimensions={0} | all-to-all | bytes 2621440 | tf_op jit(solution)/shard_map/all_to_all | solution.py:448
  181.8 0.7 sum_step.1
  (42 shorter events, 1.2 us)
Async XLA Ops:
  7.2 23.4 %copy-start.9 = (s32[256,4]{0,1:T(4,128)S(1)}, s32[256,4]{0,1:T(4,128)}, u32[]{:S(2)}) copy-start(s32[256,4]{0,1:T(4,128)} %param.10) | copy-start | bytes 12292
  7.2 77.6 %all-gather.2.cloned.1.call-start = ((), (), s32[]{:S(2)}) async-start(), calls=%async_computation.3 | async-start | bytes 2113536 | tf_op jit(solution)/shard_map/all_gather | solution.py:474
  12.6 18.0 %all-to-all-start = ((f32[16,6,8,128]{3,2,1,0:T(8,128)}), f32[16,6,8,128]{3,2,1,0:T(8,128)S(1)}, u32[]{:S(2)}, u32[]{:S(2)}) async-start(f32[16,6,8,128]{3,2,1,0:T(8,128)} %pick_points.1), calls=%async_computation | async-start | bytes 786432 | tf_op jit(solution)/shard_map/all_to_all | solution.py:448
  30.6 3.1 %collective-permute-start = (f32[16,6,8,128]{3,2,1,0:T(8,128)S(1)}, f32[16,6,8,128]{3,2,1,0:T(8,128)S(1)}, u32[]{:S(2)}, u32[]{:S(2)}) collective-permute-start(f32[16,6,8,128]{3,2,1,0:T(8,128)S(1)} %all-to-all-done.refs_0_), channel_id=1, source_target_pairs={{0,1},{1,0},{2,3},{3,2},{4,5},{5,4},{6,7},{7,6},{8,9},{9,8},{10,11... | collective-permute-start | bytes 1179656 | tf_op jit(solution)/shard_map/ppermute | solution.py:444
  31.0 1.6 copy-start
  33.7 0.8 copy-start.7
  34.4 23.0 %collective-permute-start.3 = (f32[16,6,8,128]{3,2,1,0:T(8,128)S(1)}, f32[16,6,8,128]{3,2,1,0:T(8,128)S(1)}, u32[]{:S(2)}, u32[]{:S(2)}) collective-permute-start(f32[16,6,8,128]{3,2,1,0:T(8,128)S(1)} %all-to-all-done.refs_0_), channel_id=1, source_target_pairs={{0,16},{1,17},{2,18},{3,19},{4,20},{5,21},{6,22},{7,23},{8,24},{9,... | collective-permute-start | bytes 1179656 | tf_op jit(solution)/shard_map/ppermute | solution.py:481
  37.5 20.0 %collective-permute-start.2 = (f32[16,6,8,128]{3,2,1,0:T(8,128)S(1)}, f32[16,6,8,128]{3,2,1,0:T(8,128)}, u32[]{:S(2)}, u32[]{:S(2)}) collective-permute-start(f32[16,6,8,128]{3,2,1,0:T(8,128)S(1)} %all-to-all-done.refs_0_), channel_id=1, source_target_pairs={{0,24},{1,25},{2,26},{3,27},{4,28},{5,29},{6,30},{7,31},{8,0},{9,1... | collective-permute-start | bytes 1179656 | tf_op jit(solution)/shard_map/ppermute | solution.py:481
  38.6 19.4 %collective-permute-start.1 = (f32[16,6,8,128]{3,2,1,0:T(8,128)S(1)}, f32[16,6,8,128]{3,2,1,0:T(8,128)}, u32[]{:S(2)}, u32[]{:S(2)}) collective-permute-start(f32[16,6,8,128]{3,2,1,0:T(8,128)S(1)} %all-to-all-done.refs_0_), channel_id=1, source_target_pairs={{0,8},{1,9},{2,10},{3,11},{4,12},{5,13},{6,14},{7,15},{8,16},{9,17... | collective-permute-start | bytes 1179656 | tf_op jit(solution)/shard_map/ppermute | solution.py:481
  39.5 1.0 copy-start.8
  57.4 27.4 %collective-permute-start.6 = (f32[16,6,8,128]{3,2,1,0:T(8,128)S(1)}, f32[16,6,8,128]{3,2,1,0:T(8,128)}, u32[]{:S(2)}, u32[]{:S(2)}) collective-permute-start(f32[16,6,8,128]{3,2,1,0:T(8,128)S(1)} %collective-permute-done.3.refs_2_), channel_id=1, source_target_pairs={{0,1},{1,0},{2,3},{3,2},{4,5},{5,4},{6,7},{7,6},{8,9},{9,8},{10,11... | collective-permute-start | bytes 1179656 | tf_op jit(solution)/shard_map/ppermute | solution.py:444
  57.5 27.3 %collective-permute-start.5 = (f32[16,6,8,128]{3,2,1,0:T(8,128)}, f32[16,6,8,128]{3,2,1,0:T(8,128)}, u32[]{:S(2)}, u32[]{:S(2)}) collective-permute-start(f32[16,6,8,128]{3,2,1,0:T(8,128)} %collective-permute-done.2.refs_1_), channel_id=1, source_target_pairs={{0,1},{1,0},{2,3},{3,2},{4,5},{5,4},{6,7},{7,6},{8,9},{9,8},{10,11... | collective-permute-start | bytes 1179656 | tf_op jit(solution)/shard_map/ppermute | solution.py:444
  58.0 26.8 %collective-permute-start.4 = (f32[16,6,8,128]{3,2,1,0:T(8,128)}, f32[16,6,8,128]{3,2,1,0:T(8,128)}, u32[]{:S(2)}, u32[]{:S(2)}) collective-permute-start(f32[16,6,8,128]{3,2,1,0:T(8,128)} %collective-permute-done.1.refs_0_), channel_id=1, source_target_pairs={{0,1},{1,0},{2,3},{3,2},{4,5},{5,4},{6,7},{7,6},{8,9},{9,8},{10,11... | collective-permute-start | bytes 1179656 | tf_op jit(solution)/shard_map/ppermute | solution.py:444
  84.7 27.1 %copy-start.2 = (f32[2,256,256]{2,1,0:T(8,128)S(1)}, f32[2,256,256]{2,1,0:T(8,128)}, u32[]{:S(2)}) copy-start(f32[2,256,256]{2,1,0:T(8,128)} %whitening_ref.3) | copy-start | bytes 1572868
  84.7 27.1 %copy-start.4 = (f32[2,8,256]{2,1,0:T(8,128)S(1)}, f32[2,8,256]{2,1,0:T(8,128)}, u32[]{:S(2)}) copy-start(f32[2,8,256]{2,1,0:T(8,128)} %direction_ref.7) | copy-start | bytes 49156
  84.7 27.1 %copy-start.5 = (f32[2,8,256]{2,1,0:T(8,128)S(1)}, f32[2,8,256]{2,1,0:T(8,128)}, u32[]{:S(2)}) copy-start(f32[2,8,256]{2,1,0:T(8,128)} %residual_ref.3) | copy-start | bytes 49156
  84.8 27.0 %copy-start.1 = (f32[256,8,256]{2,1,0:T(8,128)S(1)}, f32[256,8,256]{2,1,0:T(8,128)}, u32[]{:S(2)}) copy-start(f32[256,8,256]{2,1,0:T(8,128)} %all-gather.2.cloned.1.call-done.all_ref) | copy-start | bytes 6291460
  114.0 31.4 %copy-start.6 = (f32[2,8,256]{2,1,0:T(8,128)S(1)}, f32[2,8,256]{2,1,0:T(8,128)}, u32[]{:S(2)}) copy-start(f32[2,8,256]{2,1,0:T(8,128)} %solution_ref.1) | copy-start | bytes 49156
  142.3 3.2 %collective-permute-start.7 = (f32[64,5,8,128]{3,2,1,0:T(8,128)S(1)}, f32[64,5,8,128]{3,2,1,0:T(8,128)}, u32[]{:S(2)}, u32[]{:S(2)}) collective-permute-start(f32[64,5,8,128]{3,2,1,0:T(8,128)S(1)} %all_to_all.15.mine_ref), channel_id=1, source_target_pairs={{0,1},{1,0},{2,3},{3,2},{4,5},{5,4},{6,7},{7,6},{8,9},{9,8},{10,11... | collective-permute-start | bytes 3932168 | tf_op jit(solution)/shard_map/ppermute | solution.py:444
  145.4 1.0 copy-start.3
  151.9 3.1 %collective-permute-start.8 = (f32[64,5,8,128]{3,2,1,0:T(8,128)S(1)}, f32[64,5,8,128]{3,2,1,0:T(8,128)S(1)}, u32[]{:S(2)}, u32[]{:S(2)}) collective-permute-start(f32[64,5,8,128]{3,2,1,0:T(8,128)S(1)} %slice.11), channel_id=1, source_target_pairs={{0,1},{1,0},{2,3},{3,2},{4,5},{5,4},{6,7},{7,6},{8,9},{9,8},{10,11... | collective-permute-start | bytes 3932168 | tf_op jit(solution)/shard_map/ppermute | solution.py:444
Sparse Core Ops, SparseCore 0:
  11.2 68.2 all-gather.1

commit v3 on v2

--- a/solution.py
+++ b/solution.py
@@ -59,7 +59,7 @@
 
 
 def pick_points(
-    all_order, all_coordinates, direction_ref, out_ref, order_ref, coordinates_ref, sems
+    all_order, all_coordinates, direction_ref, out_ref, own_ref, order_ref, coordinates_ref, sems
 ):
     device = lax.axis_index("row") * 32 + lax.axis_index("col")
     pair = pl.multiple_of(device // 2 * PAIR, PAIR)
@@ -92,6 +92,9 @@
     for half in range(2):
         tiles.append(jnp.concatenate([found[half], found[2 + half], pad], axis=0))
 
+    for part, tile in enumerate(tiles):
+        own_ref[part] = tile
+
     def copy(i, carry):
         for part, tile in enumerate(tiles):
             out_ref[i, part] = tile
@@ -103,13 +106,16 @@
 def point_payload(ordering, coordinates, direction, copies):
     return pl.pallas_call(
         pick_points,
-        out_shape=jax.ShapeDtypeStruct((copies, 6, RHS, HALF), f32),
+        out_shape=(
+            jax.ShapeDtypeStruct((copies, 6, RHS, HALF), f32),
+            jax.ShapeDtypeStruct((6, RHS, HALF), f32),
+        ),
         in_specs=[
             pl.BlockSpec(memory_space=pltpu.HBM),
             pl.BlockSpec(memory_space=pltpu.HBM),
             pl.BlockSpec(memory_space=pltpu.VMEM),
         ],
-        out_specs=pl.BlockSpec(memory_space=pltpu.VMEM),
+        out_specs=(pl.BlockSpec(memory_space=pltpu.VMEM),) * 2,
         scratch_shapes=[
             pltpu.SMEM((PAIR,), jnp.int32),
             pltpu.VMEM(coordinates.shape, f32),
@@ -219,35 +225,22 @@
         whiten_top[b], whiten_low[b] = split2(whiten)
 
 
-def split_kernel(cross_ref, cross_top, cross_low):
-    def one(at, carry):
-        cross_top[at], cross_low[at] = split2(cross_ref[at])
-        return carry
-
-    lax.fori_loop(0, OWN * NBR, one, 0)
-
-
-def split_factors(cross):
-    vmem = pl.BlockSpec(memory_space=pltpu.VMEM)
-    return pl.pallas_call(
-        split_kernel,
-        out_shape=(jax.ShapeDtypeStruct((OWN * NBR, BS, BS), bf16),) * 2,
-        in_specs=[vmem],
-        out_specs=(vmem,) * 2,
-        compiler_params=pltpu.CompilerParams(vmem_limit_bytes=12 * MEGA),
-        cost_estimate=pl.CostEstimate(flops=4 << 20, transcendentals=0, bytes_accessed=5 << 20),
-        name="split_factors",
-    )(cross.reshape(OWN * NBR, BS, BS))
-
-
-def lower(near, valid_ref, cross_top, cross_low, field, block):
+def fetch_factors(far_cross, far_whitening, cross_ref, whitening_ref, sems):
+    copies = [
+        pltpu.make_async_copy(far_cross.at[b], cross_ref.at[b], sems.at[b]) for b in range(OWN)
+    ]
+    copies.insert(OWN, pltpu.make_async_copy(far_whitening, whitening_ref, sems.at[OWN]))
+    for copy in copies:
+        copy.start()
+    return copies
+
+
+def lower(near, valid_ref, cross_ref, field, block):
     total = field
     for k in range(NBR):
         at = block * NBR + k
         weight = valid_ref[at].astype(f32)
-        total = total - pair_dot(
-            near(at) * weight, cross_top[at], cross_low[at], ((1,), (1,))
-        )
+        total = total - pair_dot(near(at) * weight, *split2(cross_ref[block, k]), ((1,), (1,)))
     return total
 
 
@@ -256,10 +249,11 @@
 
 
 def measure_kernel(
-    list_ref, valid_ref, all_ref, residual_ref, cross_top, cross_low, whitening_ref,
-    sum_ref, direction_ref,
-    out_ref, near_ref, near_buf, whiten_top, whiten_low, sems,
+    list_ref, valid_ref, all_ref, residual_ref, far_cross, far_whitening, sum_ref, direction_ref,
+    out_ref, near_ref, near_buf, whiten_top, whiten_low, cross_ref, whitening_ref, sems,
+    factor_sems,
 ):
+    factors = fetch_factors(far_cross, far_whitening, cross_ref, whitening_ref, factor_sems)
     copies = []
     for b in range(OWN):
         for k in range(NBR):
@@ -268,15 +262,17 @@
                 pltpu.make_async_copy(all_ref.at[list_ref[at]], near_buf.at[at], sems.at[at])
             )
             copies[-1].start()
-    split_whitening(whitening_ref, whiten_top, whiten_low)
     for copy in copies:
         copy.wait()
+    factors[OWN].wait()
+    split_whitening(whitening_ref, whiten_top, whiten_low)
     old = jnp.zeros((RHS, HALF), f32)
     curvature = jnp.zeros((RHS, HALF), f32)
     tiles = []
     for b in range(OWN):
+        factors[b].wait()
         lowered = lower(
-            lambda at: near_buf[at], valid_ref, cross_top, cross_low, residual_ref[b], b
+            lambda at: near_buf[at], valid_ref, cross_ref, residual_ref[b], b
         )
         mapped = pair_dot(lowered, whiten_top[b], whiten_low[b], ((1,), (1,)))
         old = old + lanes_of(mapped * mapped)
@@ -298,35 +294,39 @@
     near_ref[...] = near_buf[...]
 
 
-def measure_step(lists, valid, gathered, residual, factors, total, direction):
+def measure_step(lists, valid, gathered, residual, cross, whitening, total, direction):
     smem = pl.BlockSpec(memory_space=pltpu.SMEM)
     vmem = pl.BlockSpec(memory_space=pltpu.VMEM)
+    far = pl.BlockSpec(memory_space=pl.ANY)
     return pl.pallas_call(
         measure_kernel,
         out_shape=(
             jax.ShapeDtypeStruct((PEERS, 5, RHS, HALF), f32),
             jax.ShapeDtypeStruct((OWN * NBR, RHS, BS), f32),
         ),
-        in_specs=[smem, smem, pl.BlockSpec(memory_space=pl.ANY)] + [vmem] * 6,
+        in_specs=[smem, smem, far, vmem, far, far, vmem, vmem],
         out_specs=(vmem, vmem),
         scratch_shapes=[
             pltpu.VMEM((OWN * NBR, RHS, BS), f32),
             pltpu.VMEM((OWN, BS, BS), bf16),
             pltpu.VMEM((OWN, BS, BS), bf16),
+            pltpu.VMEM((OWN, NBR, BS, BS), f32),
+            pltpu.VMEM((OWN, BS, BS), f32),
             pltpu.SemaphoreType.DMA((OWN * NBR,)),
+            pltpu.SemaphoreType.DMA((OWN + 1,)),
         ],
-        compiler_params=pltpu.CompilerParams(vmem_limit_bytes=8 * MEGA),
+        compiler_params=pltpu.CompilerParams(vmem_limit_bytes=57 * MEGA),
         name="measure_step",
-    )(lists, valid, gathered, residual, *factors, total, direction)
+    )(lists, valid, gathered, residual, cross, whitening, total, direction)
 
 
 def spread_kernel(
     at_ref, valid_ref, into_ref, self_ref, mine_ref, other_ref, near_ref, residual_ref, solution_ref,
-    direction_ref, cross_top, cross_low, whitening_ref,
+    direction_ref, far_cross, far_whitening,
     solution_out, residual_out, scaled_out, out_ref, old_out,
-    whiten_top, whiten_low,
+    whiten_top, whiten_low, cross_ref, whitening_ref, factor_sems,
 ):
-    split_whitening(whitening_ref, whiten_top, whiten_low)
+    factors = fetch_factors(far_cross, far_whitening, cross_ref, whitening_ref, factor_sems)
     total = jnp.zeros((RHS, HALF), f32)
     for i in range(PEERS):
         total = total + mine_ref[i, 4] + other_ref[i, 4]
@@ -347,7 +347,10 @@
         return jnp.where(((at >> 6) & 1) == 0, a, b)
 
     newer = jnp.zeros((RHS, HALF), f32)
+    factors[OWN].wait()
+    split_whitening(whitening_ref, whiten_top, whiten_low)
     for b in range(OWN):
+        factors[b].wait()
         solution_out[b] = solution_ref[b] + step * direction_ref[b]
         image = jnp.concatenate(
             [mine_ref[self_ref[0], 2 * b], mine_ref[self_ref[0], 2 * b + 1]], 1
@@ -356,7 +359,7 @@
         residual_out[b] = following
         lowered = lower(
             lambda at: near_ref[at] - step * image_of(at_ref[at]),
-            valid_ref, cross_top, cross_low, following, b,
+            valid_ref, cross_ref, following, b,
         )
         mapped = pair_dot(lowered, whiten_top[b], whiten_low[b], ((1,), (1,)))
         newer = newer + lanes_of(mapped * mapped)
@@ -364,7 +367,7 @@
         scaled_out[b] = scaled
         for k in range(NBR):
             at = b * NBR + k
-            spread = pair_dot(scaled, cross_top[at], cross_low[at], ((1,), (0,)))
+            spread = pair_dot(scaled, *split2(cross_ref[b, k]), ((1,), (0,)))
             spread = spread * valid_ref[at].astype(f32)
             to = into_ref[at]
             out_ref[to >> 1, 2 * (to & 1)] += spread[:, :HALF]
@@ -404,7 +407,7 @@
 
 
 def spread_step(
-    at, valid, into, self_at, mine, other, near, residual, solution, direction, factors
+    at, valid, into, self_at, mine, other, near, residual, solution, direction, cross, whitening
 ):
     smem = pl.BlockSpec(memory_space=pltpu.SMEM)
     vmem = pl.BlockSpec(memory_space=pltpu.VMEM)
@@ -418,16 +421,19 @@
             jax.ShapeDtypeStruct((2 * PEERS, 2 * OWN + 1, RHS, HALF), f32),
             jax.ShapeDtypeStruct((RHS, HALF), f32),
         ),
-        in_specs=[smem] * 4 + [vmem] * 9,
+        in_specs=[smem] * 4 + [vmem] * 6 + [pl.BlockSpec(memory_space=pl.ANY)] * 2,
         out_specs=(vmem,) * 5,
         scratch_shapes=[
             pltpu.VMEM((OWN, BS, BS), bf16),
             pltpu.VMEM((OWN, BS, BS), bf16),
+            pltpu.VMEM((OWN, NBR, BS, BS), f32),
+            pltpu.VMEM((OWN, BS, BS), f32),
+            pltpu.SemaphoreType.DMA((OWN + 1,)),
         ],
-        compiler_params=pltpu.CompilerParams(vmem_limit_bytes=16 * MEGA),
+        compiler_params=pltpu.CompilerParams(vmem_limit_bytes=20 * MEGA),
         name="spread_step",
     )(
-        at, valid, into, self_at, mine, other, near, residual, solution, direction, *factors
+        at, valid, into, self_at, mine, other, near, residual, solution, direction, cross, whitening
     )
 
 
@@ -473,23 +479,22 @@
 
     gathered = lax.all_gather(residual, AXES, axis=0, tiled=True)
 
-    factors = (*split_factors(cross), whitening)
-    payload = point_payload(ordering, coordinates, direction, 16)
-    own = payload[0]
+    payload, own = point_payload(ordering, coordinates, direction, 16)
     plane = exchange(payload, SAME_X_CORE)
     plane, plane_other = lax.optimization_barrier((plane, to_other_core(plane)))
     beyond = [x_around(hop)(plane) for hop in (1, 3, 2)]
     total = add_image(own, [plane, plane_other], jnp.zeros((2 * RHS, OWN * BS), f32))
     others = [to_other_core(piece) for piece in beyond]
     total = add_image(own, beyond, total)
-    total, gathered = lax.optimization_barrier((total, gathered))
     total = add_image(own, others, total)
 
-    image, near = measure_step(lists, valid, gathered, residual, factors, total, direction)
+    image, near = measure_step(
+        lists, valid, gathered, residual, cross, whitening, total, direction
+    )
     mine = exchange(image, SAME_CORE)
     other = to_other_core(mine)
     solution_next, residual_next, scaled, back, old = spread_step(
-        at, valid, into, self_at, mine, other, near, residual, solution, direction, factors
+        at, valid, into, self_at, mine, other, near, residual, solution, direction, cross, whitening
     )
     back = back[:PEERS] + to_other_core(back[PEERS:])
     direction_next = sum_step(exchange(back, SAME_CORE), scaled, direction, old)

time: 190 us -> 189 us (level)
  blocking collectives: 54.9 us -> 73.1 us
  waiting for transfers between devices: 16.5 us -> 6.97 us
  starting transfers between devices: 14.1 us -> 5.98 us
    all_to_all x2 -> x3, blocking collectives: 54.9 us -> 73.1 us  [exchange(): lax.all_to_all(value, AXES, 0, 0, axis_index_groups=groups, tiled=True)]
    all_to_all x1 -> x0, waiting for transfers between devices: 9.8 us -> none  [exchange(): lax.all_to_all(value, AXES, 0, 0, axis_index_groups=groups, tiled=True)]
    all_to_all x1 -> x0, starting transfers between devices: 8.14 us -> none  [exchange(): lax.all_to_all(value, AXES, 0, 0, axis_index_groups=groups, tiled=True)]
    pallas_call x1, Pallas kernels: 2.14 us -> 5.33 us  [measure_step(): pl.pallas_call(measure_kernel, out_shape=(jax.ShapeDtypeStruct((PEERS, 5,...]
    pallas_call x3, Pallas kernels: 70.5 us -> 67.8 us  [add_image(): pl.pallas_call(functools.partial(image_kernel, pieces), grid=(pieces * ea...]
    unnamed x20 -> x24, local copies, waits for them, and re-layouts: 4.42 us -> 2.42 us
    pallas_call x2 -> x1, Pallas kernels: 5.02 us -> 4.71 us  [point_payload(): pl.pallas_call(pick_points, out_shape=(jax.ShapeDtypeStruct((copies, 6, R...]
  transfers between devices with their start and end apart: 11 -> 10, of which waited for: 3 -> 3; matrix products, arithmetic and copies ran while one was open for 1% -> 1% of each run, Pallas kernels for 26% -> 38%
where the time goes in v3:
time: 189 us
  Pallas kernels  84.1 us (44%)
  blocking collectives  73.1 us (39%)
  between operations  14.3 us (8%)
  waiting for transfers between devices  6.97 us (4%)
  starting transfers between devices  5.98 us (3%)
  local copies, waits for them, and re-layouts  3.88 us (2%)
    all_to_all x3, blocking collectives, exchange(): lax.all_to_all(value, AXES, 0, 0, axis_index_groups=groups, tiled=True)  73.1 us
    pallas_call x3, Pallas kernels, add_image(): pl.pallas_call(functools.partial(image_kernel, pieces), grid=(pieces * ea...  67.8 us
    ppermute x6, waiting for transfers between devices, to_other_core(): return lax.ppermute(value, 'col', [(i, i ^ 1) for i in range(32)])  6.28 us
    pallas_call x1, Pallas kernels, spread_step(): pl.pallas_call(spread_kernel, out_shape=(own, own, own, jax.ShapeDtypeStr...  5.56 us
    pallas_call x1, Pallas kernels, measure_step(): pl.pallas_call(measure_kernel, out_shape=(jax.ShapeDtypeStruct((PEERS, 5,...  5.33 us
    ppermute x3, starting transfers between devices, per_device(): beyond = [x_around(hop)(plane) for hop in (1, 3, 2)]  5.05 us
    pallas_call x1, Pallas kernels, point_payload(): pl.pallas_call(pick_points, out_shape=(jax.ShapeDtypeStruct((copies, 6, R...  4.71 us
  transfers between devices with their start and end apart: 10, of which 3 were waited for; matrix products, arithmetic and copies ran while one was open for 1% of the time, Pallas kernels for 38%

profile of v3, /device:TPU:0, one launch (start us, length us, event | category | flops | bytes accessed | tf_op | source)
XLA Modules:
  0.0 188.6 jit_solution(205486415191785761)
XLA Ops:
  7.2 0.7 all-gather.2.cloned.1.call-update
  7.9 4.7 %pick_points.1 = (f32[16,6,8,128]{3,2,1,0:T(8,128)}, f32[6,8,128]{2,1,0:T(8,128)}) custom-call(s32[65536]{0:T(1024)} %all_order.1, f32[3,65536]{1,0:T(4,128)} %all_coordinates.1, f32[2,8,256]{2,1,0:T(8,128)} %direction_ref.7), custom_call_target="tpu_custom_call" | custom-call | tf_op jit(solution)/shard_map/pick_points/pallas_call | solution.py:107
  12.6 18.0 %all_to_all.15.refs_0_ = f32[16,6,8,128]{3,2,1,0:T(8,128)S(1)} all-to-all(f32[16,6,8,128]{3,2,1,0:T(8,128)} %get-tuple-element.15), channel_id=1, replica_groups={{0,2,4,6,32,34,36,38,64,66,68,70,96,98,100,102},{1,3,5,7,33,35,37,39,65..., dimensions={0} | all-to-all | bytes 786432 | tf_op jit(solution)/shard_map/all_to_all | solution.py:454
  30.8 0.6 reshape.22.valid_ref
  31.5 0.6 reshape.18.list_ref
  32.1 0.3 collective-permute-done.refs_1_
  32.3 3.0 %collective-permute-start.3 = (f32[16,6,8,128]{3,2,1,0:T(8,128)S(1)}, f32[16,6,8,128]{3,2,1,0:T(8,128)S(1)}, u32[]{:S(2)}, u32[]{:S(2)}) collective-permute-start(f32[16,6,8,128]{3,2,1,0:T(8,128)S(1)} %all_to_all.15.refs_0_), channel_id=1, source_target_pairs={{0,16},{1,17},{2,18},{3,19},{4,20},{5,21},{6,22},{7,23},{8,24},{9,... | collective-permute-start | bytes 1179656 | tf_op jit(solution)/shard_map/ppermute | solution.py:485
  35.3 1.1 collective-permute-start.2
  36.5 0.9 collective-permute-start.1
  37.4 0.7 copy-done.8
  38.1 16.9 %image.3.start_ref = f32[16,512]{1,0:T(8,128)S(1)} custom-call(f32[6,8,128]{2,1,0:T(8,128)S(1)} %copy-done.8, f32[16,512]{1,0:T(8,128)S(1)} %broadcast_in_dim.8.start_ref, f32[16,6,8,128]{3,2,1,0:T(8,128)S(1)} %all_to_all.15.refs_0_, f32[16,6,8,128]{3,2,1,0:T(8,128)S(1)} %collective-permute-done.refs_1_), custom_call_target="tpu_custom_call" | custom-call | flops 5033164800 | bytes 786432 | tf_op jit(solution)/shard_map/image/pallas_call | solution.py:196
  55.1 0.5 collective-permute-start.5
  55.7 25.4 %image.4.start_ref = f32[16,512]{1,0:T(8,128)S(1)} custom-call(f32[6,8,128]{2,1,0:T(8,128)S(1)} %copy-done.9, f32[16,512]{1,0:T(8,128)S(1)} %image.3.start_ref, f32[16,6,8,128]{3,2,1,0:T(8,128)S(1)} %collective-permute-done.1.refs_0_, f32[16,6,8,128]{3,2,1,0:T(8,128)S(1)} %collective-permute-done.2.refs_1_, f32[16,6,8,128]{3,2,1,0:T(8,128)S(1)} %collective-permute-done.3.refs_2_), custom_call_target="tpu_custom_call" | custom-call | flops 7549747200 | bytes 1179648 | tf_op jit(solution)/shard_map/image/pallas_call | solution.py:196
  81.2 25.5 %image.5.sum_ref = f32[16,512]{1,0:T(8,128)S(1)} custom-call(f32[6,8,128]{2,1,0:T(8,128)S(1)} %copy-done.9, f32[16,512]{1,0:T(8,128)S(1)} %image.4.start_ref, f32[16,6,8,128]{3,2,1,0:T(8,128)S(1)} %collective-permute-done.4.refs_0_, f32[16,6,8,128]{3,2,1,0:T(8,128)S(1)} %collective-permute-done.5.refs_1_, f32[16,6,8,128]{3,2,1,0:T(8,128)S(1)} %collective-permute-done.6.refs_2_), custom_call_target="tpu_custom_call" | custom-call | flops 7549747200 | bytes 1179648 | tf_op jit(solution)/shard_map/image/pallas_call | solution.py:196
  106.7 0.6 copy-done.5
  107.3 5.3 %measure_step.1 = (f32[64,5,8,128]{3,2,1,0:T(8,128)}, f32[8,8,256]{2,1,0:T(8,128)}) custom-call(s32[8]{0:T(128)} %reshape.18.list_ref, s32[8]{0:T(128)} %reshape.22.valid_ref, f32[256,8,256]{2,1,0:T(8,128)} %all-gather.2.cloned.1.call-done.all_ref, f32[2,8,256]{2,1,0:T(8,128)} %residual_ref.3, f32[2,4,256,256]{3,2,1,0:T(8,128)} %far_cross.3, ...), custom_call_target="tpu_custom_call" | custom-call | tf_op jit(solution)/shard_map/measure_step/pallas_call | solution.py:301
  112.7 28.6 %all_to_all.16.mine_ref = f32[64,5,8,128]{3,2,1,0:T(8,128)S(1)} all-to-all(f32[64,5,8,128]{3,2,1,0:T(8,128)} %get-tuple-element.18), channel_id=1, replica_groups={{0,2,4,6,8,10,12,14,16,18,20,22,24,26,28,30,32,34,36,38,40,42,44,46,48,..., dimensions={0} | all-to-all | bytes 2621440 | tf_op jit(solution)/shard_map/all_to_all | solution.py:454
  141.3 3.1 %collective-permute-done.7.other_ref = f32[64,5,8,128]{3,2,1,0:T(8,128)} collective-permute-done((f32[64,5,8,128]{3,2,1,0:T(8,128)S(1)}, f32[64,5,8,128]{3,2,1,0:T(8,128)}, u32[]{:S(2)}, u32[]{:S(2)}) %collective-permute-start.7) | collective-permute-done | bytes 1310752 | tf_op jit(solution)/shard_map/ppermute | solution.py:450
  144.5 1.0 copy-done.1
  145.5 5.6 %spread_step.1 = (f32[2,8,256]{2,1,0:T(8,128)}, f32[2,8,256]{2,1,0:T(8,128)}, f32[2,8,256]{2,1,0:T(8,128)S(1)}, f32[128,5,8,128]{3,2,1,0:T(8,128)S(1)}, f32[8,128]{1,0:T(8,128)S(1)}) custom-call(s32[8]{0:T(128)S(1)} %multiply_add_fusion.1.at_ref, s32[8]{0:T(128)S(1)} %copy-done.7, s32[8]{0:T(128)S(1)} %get-tuple-element.25.into_ref, s32[1]{0:T(128)} %bitcast.self_ref, ...), custom_call_target="tpu_custom_call" | custom-call | tf_op jit(solution)/shard_map/spread_step/pallas_call | solution.py:415
  151.2 0.2 collective-permute-start.8
  151.4 2.9 %collective-permute-done.8 = f32[64,5,8,128]{3,2,1,0:T(8,128)S(1)} collective-permute-done((f32[64,5,8,128]{3,2,1,0:T(8,128)S(1)}, f32[64,5,8,128]{3,2,1,0:T(8,128)S(1)}, u32[]{:S(2)}, u32[]{:S(2)}) %collective-permute-start.8) | collective-permute-done | bytes 1310752 | tf_op jit(solution)/shard_map/ppermute | solution.py:450
  154.4 26.5 %all_to_all.17.all_ref = f32[64,5,8,128]{3,2,1,0:T(8,128)S(1)} all-to-all(f32[64,5,8,128]{3,2,1,0:T(8,128)S(1)} %slice_add_fusion), channel_id=1, replica_groups={{0,2,4,6,8,10,12,14,16,18,20,22,24,26,28,30,32,34,36,38,40,42,44,46,48,..., dimensions={0} | all-to-all | bytes 2621440 | tf_op jit(solution)/shard_map/all_to_all | solution.py:454
  181.0 0.7 sum_step.1
  (43 shorter events, 0.8 us)
Async XLA Ops:
  7.2 23.4 %copy-start.10 = (s32[256,4]{0,1:T(4,128)S(1)}, s32[256,4]{0,1:T(4,128)}, u32[]{:S(2)}) copy-start(s32[256,4]{0,1:T(4,128)} %param.10) | copy-start | bytes 12292
  7.2 100.1 %all-gather.2.cloned.1.call-start = ((), (), s32[]{:S(2)}) async-start(), calls=%async_computation.3 | async-start | bytes 2113536 | tf_op jit(solution)/shard_map/all_gather | solution.py:480
  30.6 1.7 collective-permute-start
  32.3 22.7 %collective-permute-start.3 = (f32[16,6,8,128]{3,2,1,0:T(8,128)S(1)}, f32[16,6,8,128]{3,2,1,0:T(8,128)S(1)}, u32[]{:S(2)}, u32[]{:S(2)}) collective-permute-start(f32[16,6,8,128]{3,2,1,0:T(8,128)S(1)} %all_to_all.15.refs_0_), channel_id=1, source_target_pairs={{0,16},{1,17},{2,18},{3,19},{4,20},{5,21},{6,22},{7,23},{8,24},{9,... | collective-permute-start | bytes 1179656 | tf_op jit(solution)/shard_map/ppermute | solution.py:485
  35.3 19.8 %collective-permute-start.2 = (f32[16,6,8,128]{3,2,1,0:T(8,128)S(1)}, f32[16,6,8,128]{3,2,1,0:T(8,128)S(1)}, u32[]{:S(2)}, u32[]{:S(2)}) collective-permute-start(f32[16,6,8,128]{3,2,1,0:T(8,128)S(1)} %all_to_all.15.refs_0_), channel_id=1, source_target_pairs={{0,24},{1,25},{2,26},{3,27},{4,28},{5,29},{6,30},{7,31},{8,0},{9,1... | collective-permute-start | bytes 1179656 | tf_op jit(solution)/shard_map/ppermute | solution.py:485
  36.5 19.1 %collective-permute-start.1 = (f32[16,6,8,128]{3,2,1,0:T(8,128)S(1)}, f32[16,6,8,128]{3,2,1,0:T(8,128)S(1)}, u32[]{:S(2)}, u32[]{:S(2)}) collective-permute-start(f32[16,6,8,128]{3,2,1,0:T(8,128)S(1)} %all_to_all.15.refs_0_), channel_id=1, source_target_pairs={{0,8},{1,9},{2,10},{3,11},{4,12},{5,13},{6,14},{7,15},{8,16},{9,17... | collective-permute-start | bytes 1179656 | tf_op jit(solution)/shard_map/ppermute | solution.py:485
  37.4 0.7 copy-start.8
  38.1 17.6 %copy-start.9 = (f32[6,8,128]{2,1,0:T(8,128)S(1)}, f32[6,8,128]{2,1,0:T(8,128)}, u32[]{:S(2)}) copy-start(f32[6,8,128]{2,1,0:T(8,128)} %get-tuple-element.14.own_ref) | copy-start | bytes 73732
  55.0 26.1 %collective-permute-start.6 = (f32[16,6,8,128]{3,2,1,0:T(8,128)S(1)}, f32[16,6,8,128]{3,2,1,0:T(8,128)S(1)}, u32[]{:S(2)}, u32[]{:S(2)}) collective-permute-start(f32[16,6,8,128]{3,2,1,0:T(8,128)S(1)} %collective-permute-done.3.refs_2_), channel_id=1, source_target_pairs={{0,1},{1,0},{2,3},{3,2},{4,5},{5,4},{6,7},{7,6},{8,9},{9,8},{10,11... | collective-permute-start | bytes 1179656 | tf_op jit(solution)/shard_map/ppermute | solution.py:450
  55.1 26.0 %collective-permute-start.5 = (f32[16,6,8,128]{3,2,1,0:T(8,128)S(1)}, f32[16,6,8,128]{3,2,1,0:T(8,128)S(1)}, u32[]{:S(2)}, u32[]{:S(2)}) collective-permute-start(f32[16,6,8,128]{3,2,1,0:T(8,128)S(1)} %collective-permute-done.2.refs_1_), channel_id=1, source_target_pairs={{0,1},{1,0},{2,3},{3,2},{4,5},{5,4},{6,7},{7,6},{8,9},{9,8},{10,11... | collective-permute-start | bytes 1179656 | tf_op jit(solution)/shard_map/ppermute | solution.py:450
  55.6 25.6 %collective-permute-start.4 = (f32[16,6,8,128]{3,2,1,0:T(8,128)S(1)}, f32[16,6,8,128]{3,2,1,0:T(8,128)S(1)}, u32[]{:S(2)}, u32[]{:S(2)}) collective-permute-start(f32[16,6,8,128]{3,2,1,0:T(8,128)S(1)} %collective-permute-done.1.refs_0_), channel_id=1, source_target_pairs={{0,1},{1,0},{2,3},{3,2},{4,5},{5,4},{6,7},{7,6},{8,9},{9,8},{10,11... | collective-permute-start | bytes 1179656 | tf_op jit(solution)/shard_map/ppermute | solution.py:450
  106.7 0.6 copy-start.5
  112.6 28.6 %copy-start.11 = (s32[8]{0:T(128)S(1)}, s32[8]{0:T(128)}, u32[]{:S(2)}) copy-start(s32[8]{0:T(128)} %reshape.18.list_ref) | copy-start | bytes 100
  112.6 31.8 %copy-start = (f32[2,4,256,256]{3,2,1,0:T(8,128)S(1)}, f32[2,4,256,256]{3,2,1,0:T(8,128)}, u32[]{:S(2)}) copy-start(f32[2,4,256,256]{3,2,1,0:T(8,128)} %far_cross.3) | copy-start | bytes 6291460
  112.6 31.8 %copy-start.2 = (f32[2,8,256]{2,1,0:T(8,128)S(1)}, f32[2,8,256]{2,1,0:T(8,128)}, u32[]{:S(2)}) copy-start(f32[2,8,256]{2,1,0:T(8,128)} %direction_ref.7) | copy-start | bytes 49156
  112.6 31.8 %copy-start.3 = (f32[2,8,256]{2,1,0:T(8,128)S(1)}, f32[2,8,256]{2,1,0:T(8,128)}, u32[]{:S(2)}) copy-start(f32[2,8,256]{2,1,0:T(8,128)} %residual_ref.3) | copy-start | bytes 49156
  112.7 31.8 %copy-start.4 = (f32[8,8,256]{2,1,0:T(8,128)S(1)}, f32[8,8,256]{2,1,0:T(8,128)}, u32[]{:S(2)}) copy-start(f32[8,8,256]{2,1,0:T(8,128)} %get-tuple-element.19.near_ref) | copy-start | bytes 196612
  112.7 31.8 %copy-start.6 = (f32[2,8,256]{2,1,0:T(8,128)S(1)}, f32[2,8,256]{2,1,0:T(8,128)}, u32[]{:S(2)}) copy-start(f32[2,8,256]{2,1,0:T(8,128)} %solution_ref.1) | copy-start | bytes 49156
  112.7 31.8 %copy-start.7 = (s32[8]{0:T(128)S(1)}, s32[8]{0:T(128)}, u32[]{:S(2)}) copy-start(s32[8]{0:T(128)} %reshape.22.valid_ref) | copy-start | bytes 100
  141.3 3.2 %collective-permute-start.7 = (f32[64,5,8,128]{3,2,1,0:T(8,128)S(1)}, f32[64,5,8,128]{3,2,1,0:T(8,128)}, u32[]{:S(2)}, u32[]{:S(2)}) collective-permute-start(f32[64,5,8,128]{3,2,1,0:T(8,128)S(1)} %all_to_all.16.mine_ref), channel_id=1, source_target_pairs={{0,1},{1,0},{2,3},{3,2},{4,5},{5,4},{6,7},{7,6},{8,9},{9,8},{10,11... | collective-permute-start | bytes 3932168 | tf_op jit(solution)/shard_map/ppermute | solution.py:450
  144.5 1.0 copy-start.1
  151.2 3.1 %collective-permute-start.8 = (f32[64,5,8,128]{3,2,1,0:T(8,128)S(1)}, f32[64,5,8,128]{3,2,1,0:T(8,128)S(1)}, u32[]{:S(2)}, u32[]{:S(2)}) collective-permute-start(f32[64,5,8,128]{3,2,1,0:T(8,128)S(1)} %slice.7), channel_id=1, source_target_pairs={{0,1},{1,0},{2,3},{3,2},{4,5},{5,4},{6,7},{7,6},{8,9},{9,8},{10,11... | collective-permute-start | bytes 3932168 | tf_op jit(solution)/shard_map/ppermute | solution.py:450
Sparse Core Ops, SparseCore 0:
  11.2 73.2 all-gather.1

commit v4 on v3

--- a/solution.py
+++ b/solution.py
@@ -19,6 +19,7 @@
 HALF = 128
 STEP = 4
 PEERS = 64
+GUARD = 2.0**-20
 PAIR = 2 * OWN * BS
 MEGA = 1 << 20
 
@@ -171,8 +172,7 @@
                 x = square[
                     job % 2, part * BS : (part + 1) * BS, lanes * HALF : (lanes + 1) * HALF
                 ]
-                x = jnp.maximum(x, 1e-30)
-                u = -offset - x * lax.rsqrt(x)
+                u = -offset - x * lax.rsqrt(jnp.maximum(x, GUARD))
                 tile = u * jnp.exp2(u)
                 top, low = split2(tile)
                 field = field_part[q * (TALL // BS) + part]
@@ -315,7 +315,7 @@
             pltpu.SemaphoreType.DMA((OWN * NBR,)),
             pltpu.SemaphoreType.DMA((OWN + 1,)),
         ],
-        compiler_params=pltpu.CompilerParams(vmem_limit_bytes=57 * MEGA),
+        compiler_params=pltpu.CompilerParams(vmem_limit_bytes=12 * MEGA),
         name="measure_step",
     )(lists, valid, gathered, residual, cross, whitening, total, direction)
 

time: 189 us -> 183 us (0.968)
  Pallas kernels: 84.1 us -> 76.9 us
    pallas_call x3, Pallas kernels: 67.8 us -> 63.4 us  [add_image(): pl.pallas_call(functools.partial(image_kernel, pieces), grid=(pieces * ea...]
    pallas_call x1, Pallas kernels: 5.33 us -> 2.47 us  [measure_step(): pl.pallas_call(measure_kernel, out_shape=(jax.ShapeDtypeStruct((PEERS, 5,...]
  transfers between devices with their start and end apart: 10 -> 10, of which waited for: 3 -> 3; matrix products, arithmetic and copies ran while one was open for 1% -> 0% of each run, Pallas kernels for 38% -> 37%
where the time goes in v4:
time: 183 us; the launch traced here: 182 us
  Pallas kernels  76.9 us (42%)
  blocking collectives  72.8 us (40%)
  between operations  14.3 us (8%)
  waiting for transfers between devices  8 us (4%)
  starting transfers between devices  5.98 us (3%)
  local copies, waits for them, and re-layouts  3.85 us (2%)
    all_to_all x3, blocking collectives, exchange(): lax.all_to_all(value, AXES, 0, 0, axis_index_groups=groups, tiled=True)  72.8 us
    pallas_call x3, Pallas kernels, add_image(): pl.pallas_call(functools.partial(image_kernel, pieces), grid=(pieces * ea...  63.4 us
    ppermute x6, waiting for transfers between devices, to_other_core(): return lax.ppermute(value, 'col', [(i, i ^ 1) for i in range(32)])  7.29 us
    pallas_call x1, Pallas kernels, spread_step(): pl.pallas_call(spread_kernel, out_shape=(own, own, own, jax.ShapeDtypeStr...  5.56 us
    ppermute x3, starting transfers between devices, per_device(): beyond = [x_around(hop)(plane) for hop in (1, 3, 2)]  5.05 us
    pallas_call x1, Pallas kernels, point_payload(): pl.pallas_call(pick_points, out_shape=(jax.ShapeDtypeStruct((copies, 6, R...  4.7 us
  transfers between devices with their start and end apart: 10, of which 3 were waited for; matrix products, arithmetic and copies ran while one was open for 0% of the time, Pallas kernels for 37%

profile of v4, /device:TPU:0, one launch (start us, length us, event | category | flops | bytes accessed | tf_op | source)
XLA Modules:
  0.0 182.1 jit_solution(6440560274817847058)
XLA Ops:
  7.2 0.7 all-gather.2.cloned.1.call-update
  7.9 4.7 %pick_points.1 = (f32[16,6,8,128]{3,2,1,0:T(8,128)}, f32[6,8,128]{2,1,0:T(8,128)}) custom-call(s32[65536]{0:T(1024)} %all_order.1, f32[3,65536]{1,0:T(4,128)} %all_coordinates.1, f32[2,8,256]{2,1,0:T(8,128)} %direction_ref.7), custom_call_target="tpu_custom_call" | custom-call | tf_op jit(solution)/shard_map/pick_points/pallas_call | solution.py:108
  12.6 18.0 %all_to_all.15.refs_0_ = f32[16,6,8,128]{3,2,1,0:T(8,128)S(1)} all-to-all(f32[16,6,8,128]{3,2,1,0:T(8,128)} %get-tuple-element.15), channel_id=1, replica_groups={{0,2,4,6,32,34,36,38,64,66,68,70,96,98,100,102},{1,3,5,7,33,35,37,39,65..., dimensions={0} | all-to-all | bytes 786432 | tf_op jit(solution)/shard_map/all_to_all | solution.py:454
  31.0 1.3 collective-permute-done.refs_1_
  32.3 3.0 %collective-permute-start.3 = (f32[16,6,8,128]{3,2,1,0:T(8,128)S(1)}, f32[16,6,8,128]{3,2,1,0:T(8,128)S(1)}, u32[]{:S(2)}, u32[]{:S(2)}) collective-permute-start(f32[16,6,8,128]{3,2,1,0:T(8,128)S(1)} %all_to_all.15.refs_0_), channel_id=1, source_target_pairs={{0,16},{1,17},{2,18},{3,19},{4,20},{5,21},{6,22},{7,23},{8,24},{9,... | collective-permute-start | bytes 1179656 | tf_op jit(solution)/shard_map/ppermute | solution.py:485
  35.3 1.1 collective-permute-start.2
  36.5 0.9 collective-permute-start.1
  37.4 0.7 copy-done.7
  38.1 15.9 %image.3.start_ref = f32[16,512]{1,0:T(8,128)S(1)} custom-call(f32[6,8,128]{2,1,0:T(8,128)S(1)} %copy-done.7, f32[16,512]{1,0:T(8,128)S(1)} %broadcast_in_dim.8.start_ref, f32[16,6,8,128]{3,2,1,0:T(8,128)S(1)} %all_to_all.15.refs_0_, f32[16,6,8,128]{3,2,1,0:T(8,128)S(1)} %collective-permute-done.refs_1_), custom_call_target="tpu_custom_call" | custom-call | flops 5033164800 | bytes 786432 | tf_op jit(solution)/shard_map/image/pallas_call | solution.py:196
  54.1 0.5 collective-permute-start.5
  54.6 0.1 collective-permute-start.4
  54.7 23.8 %image.4.start_ref = f32[16,512]{1,0:T(8,128)S(1)} custom-call(f32[6,8,128]{2,1,0:T(8,128)S(1)} %copy-done.7, f32[16,512]{1,0:T(8,128)S(1)} %image.3.start_ref, f32[16,6,8,128]{3,2,1,0:T(8,128)S(1)} %collective-permute-done.1.refs_0_, f32[16,6,8,128]{3,2,1,0:T(8,128)S(1)} %collective-permute-done.2.refs_1_, f32[16,6,8,128]{3,2,1,0:T(8,128)S(1)} %collective-permute-done.3.refs_2_), custom_call_target="tpu_custom_call" | custom-call | flops 7549747200 | bytes 1179648 | tf_op jit(solution)/shard_map/image/pallas_call | solution.py:196
  78.6 23.8 %image.5.sum_ref = f32[16,512]{1,0:T(8,128)S(1)} custom-call(f32[6,8,128]{2,1,0:T(8,128)S(1)} %copy-done.8, f32[16,512]{1,0:T(8,128)S(1)} %image.4.start_ref, f32[16,6,8,128]{3,2,1,0:T(8,128)S(1)} %collective-permute-done.4.refs_0_, f32[16,6,8,128]{3,2,1,0:T(8,128)S(1)} %collective-permute-done.5.refs_1_, f32[16,6,8,128]{3,2,1,0:T(8,128)S(1)} %collective-permute-done.6.refs_2_), custom_call_target="tpu_custom_call" | custom-call | flops 7549747200 | bytes 1179648 | tf_op jit(solution)/shard_map/image/pallas_call | solution.py:196
  102.4 1.6 copy-done.1
  104.0 2.5 %measure_step.1 = (f32[64,5,8,128]{3,2,1,0:T(8,128)S(1)}, f32[8,8,256]{2,1,0:T(8,128)S(1)}) custom-call(s32[8]{0:T(128)S(1)} %reshape.18.list_ref, s32[8]{0:T(128)S(1)} %reshape.22.valid_ref, f32[256,8,256]{2,1,0:T(8,128)S(1)} %copy-done.1, f32[2,8,256]{2,1,0:T(8,128)S(1)} %copy-done.5, f32[2,4,256,256]{3,2,1,0:T(8,128)S(1)} %copy-done, ...), custom_call_target="tpu_custom_call" | custom-call | tf_op jit(solution)/shard_map/measure_step/pallas_call | solution.py:301
  106.5 28.3 %all_to_all.16.mine_ref = f32[64,5,8,128]{3,2,1,0:T(8,128)S(1)} all-to-all(f32[64,5,8,128]{3,2,1,0:T(8,128)S(1)} %get-tuple-element.18), channel_id=1, replica_groups={{0,2,4,6,8,10,12,14,16,18,20,22,24,26,28,30,32,34,36,38,40,42,44,46,48,..., dimensions={0} | all-to-all | bytes 2621440 | tf_op jit(solution)/shard_map/all_to_all | solution.py:454
  134.8 3.1 %collective-permute-done.7.other_ref = f32[64,5,8,128]{3,2,1,0:T(8,128)} collective-permute-done((f32[64,5,8,128]{3,2,1,0:T(8,128)S(1)}, f32[64,5,8,128]{3,2,1,0:T(8,128)}, u32[]{:S(2)}, u32[]{:S(2)}) %collective-permute-start.7) | collective-permute-done | bytes 1310752 | tf_op jit(solution)/shard_map/ppermute | solution.py:450
  138.0 1.0 copy-done.3
  139.0 5.6 %spread_step.1 = (f32[2,8,256]{2,1,0:T(8,128)}, f32[2,8,256]{2,1,0:T(8,128)}, f32[2,8,256]{2,1,0:T(8,128)S(1)}, f32[128,5,8,128]{3,2,1,0:T(8,128)S(1)}, f32[8,128]{1,0:T(8,128)S(1)}) custom-call(s32[8]{0:T(128)S(1)} %multiply_add_fusion.1.at_ref, s32[8]{0:T(128)S(1)} %reshape.22.valid_ref, s32[8]{0:T(128)S(1)} %get-tuple-element.25.into_ref, ...), custom_call_target="tpu_custom_call" | custom-call | tf_op jit(solution)/shard_map/spread_step/pallas_call | solution.py:415
  144.7 0.2 collective-permute-start.8
  144.9 2.9 %collective-permute-done.8 = f32[64,5,8,128]{3,2,1,0:T(8,128)S(1)} collective-permute-done((f32[64,5,8,128]{3,2,1,0:T(8,128)S(1)}, f32[64,5,8,128]{3,2,1,0:T(8,128)S(1)}, u32[]{:S(2)}, u32[]{:S(2)}) %collective-permute-start.8) | collective-permute-done | bytes 1310752 | tf_op jit(solution)/shard_map/ppermute | solution.py:450
  147.8 0.1 slice_add_fusion
  147.9 26.6 %all_to_all.17.all_ref = f32[64,5,8,128]{3,2,1,0:T(8,128)S(1)} all-to-all(f32[64,5,8,128]{3,2,1,0:T(8,128)S(1)} %slice_add_fusion), channel_id=1, replica_groups={{0,2,4,6,8,10,12,14,16,18,20,22,24,26,28,30,32,34,36,38,40,42,44,46,48,..., dimensions={0} | all-to-all | bytes 2621440 | tf_op jit(solution)/shard_map/all_to_all | solution.py:454
  174.5 0.7 sum_step.1
  (39 shorter events, 0.8 us)
Async XLA Ops:
  7.2 23.4 %copy-start.9 = (s32[256,4]{0,1:T(4,128)S(1)}, s32[256,4]{0,1:T(4,128)}, u32[]{:S(2)}) copy-start(s32[256,4]{0,1:T(4,128)} %param.10) | copy-start | bytes 12292
  7.2 95.2 %all-gather.2.cloned.1.call-start = ((), (), s32[]{:S(2)}) async-start(), calls=%async_computation.3 | async-start | bytes 2113536 | tf_op jit(solution)/shard_map/all_gather | solution.py:480
  30.6 1.7 collective-permute-start
  32.3 21.7 %collective-permute-start.3 = (f32[16,6,8,128]{3,2,1,0:T(8,128)S(1)}, f32[16,6,8,128]{3,2,1,0:T(8,128)S(1)}, u32[]{:S(2)}, u32[]{:S(2)}) collective-permute-start(f32[16,6,8,128]{3,2,1,0:T(8,128)S(1)} %all_to_all.15.refs_0_), channel_id=1, source_target_pairs={{0,16},{1,17},{2,18},{3,19},{4,20},{5,21},{6,22},{7,23},{8,24},{9,... | collective-permute-start | bytes 1179656 | tf_op jit(solution)/shard_map/ppermute | solution.py:485
  35.3 18.8 %collective-permute-start.2 = (f32[16,6,8,128]{3,2,1,0:T(8,128)S(1)}, f32[16,6,8,128]{3,2,1,0:T(8,128)S(1)}, u32[]{:S(2)}, u32[]{:S(2)}) collective-permute-start(f32[16,6,8,128]{3,2,1,0:T(8,128)S(1)} %all_to_all.15.refs_0_), channel_id=1, source_target_pairs={{0,24},{1,25},{2,26},{3,27},{4,28},{5,29},{6,30},{7,31},{8,0},{9,1... | collective-permute-start | bytes 1179656 | tf_op jit(solution)/shard_map/ppermute | solution.py:485
  36.5 18.1 %collective-permute-start.1 = (f32[16,6,8,128]{3,2,1,0:T(8,128)S(1)}, f32[16,6,8,128]{3,2,1,0:T(8,128)S(1)}, u32[]{:S(2)}, u32[]{:S(2)}) collective-permute-start(f32[16,6,8,128]{3,2,1,0:T(8,128)S(1)} %all_to_all.15.refs_0_), channel_id=1, source_target_pairs={{0,8},{1,9},{2,10},{3,11},{4,12},{5,13},{6,14},{7,15},{8,16},{9,17... | collective-permute-start | bytes 1179656 | tf_op jit(solution)/shard_map/ppermute | solution.py:485
  37.4 0.7 copy-start.7
  54.0 24.6 %copy-start.8 = (f32[6,8,128]{2,1,0:T(8,128)S(1)}, f32[6,8,128]{2,1,0:T(8,128)}, u32[]{:S(2)}) copy-start(f32[6,8,128]{2,1,0:T(8,128)} %get-tuple-element.14.own_ref) | copy-start | bytes 73732
  54.0 24.6 %collective-permute-start.6 = (f32[16,6,8,128]{3,2,1,0:T(8,128)S(1)}, f32[16,6,8,128]{3,2,1,0:T(8,128)S(1)}, u32[]{:S(2)}, u32[]{:S(2)}) collective-permute-start(f32[16,6,8,128]{3,2,1,0:T(8,128)S(1)} %collective-permute-done.3.refs_2_), channel_id=1, source_target_pairs={{0,1},{1,0},{2,3},{3,2},{4,5},{5,4},{6,7},{7,6},{8,9},{9,8},{10,11... | collective-permute-start | bytes 1179656 | tf_op jit(solution)/shard_map/ppermute | solution.py:450
  54.1 24.5 %collective-permute-start.5 = (f32[16,6,8,128]{3,2,1,0:T(8,128)S(1)}, f32[16,6,8,128]{3,2,1,0:T(8,128)S(1)}, u32[]{:S(2)}, u32[]{:S(2)}) collective-permute-start(f32[16,6,8,128]{3,2,1,0:T(8,128)S(1)} %collective-permute-done.2.refs_1_), channel_id=1, source_target_pairs={{0,1},{1,0},{2,3},{3,2},{4,5},{5,4},{6,7},{7,6},{8,9},{9,8},{10,11... | collective-permute-start | bytes 1179656 | tf_op jit(solution)/shard_map/ppermute | solution.py:450
  54.6 24.0 %collective-permute-start.4 = (f32[16,6,8,128]{3,2,1,0:T(8,128)S(1)}, f32[16,6,8,128]{3,2,1,0:T(8,128)S(1)}, u32[]{:S(2)}, u32[]{:S(2)}) collective-permute-start(f32[16,6,8,128]{3,2,1,0:T(8,128)S(1)} %collective-permute-done.1.refs_0_), channel_id=1, source_target_pairs={{0,1},{1,0},{2,3},{3,2},{4,5},{5,4},{6,7},{7,6},{8,9},{9,8},{10,11... | collective-permute-start | bytes 1179656 | tf_op jit(solution)/shard_map/ppermute | solution.py:450
  78.5 23.9 %copy-start.2 = (f32[2,256,256]{2,1,0:T(8,128)S(1)}, f32[2,256,256]{2,1,0:T(8,128)}, u32[]{:S(2)}) copy-start(f32[2,256,256]{2,1,0:T(8,128)} %far_whitening.3) | copy-start | bytes 1572868
  78.5 23.9 %copy-start.4 = (f32[2,8,256]{2,1,0:T(8,128)S(1)}, f32[2,8,256]{2,1,0:T(8,128)}, u32[]{:S(2)}) copy-start(f32[2,8,256]{2,1,0:T(8,128)} %direction_ref.7) | copy-start | bytes 49156
  78.5 23.9 %copy-start.5 = (f32[2,8,256]{2,1,0:T(8,128)S(1)}, f32[2,8,256]{2,1,0:T(8,128)}, u32[]{:S(2)}) copy-start(f32[2,8,256]{2,1,0:T(8,128)} %residual_ref.3) | copy-start | bytes 49156
  78.6 23.8 %copy-start = (f32[2,4,256,256]{3,2,1,0:T(8,128)S(1)}, f32[2,4,256,256]{3,2,1,0:T(8,128)}, u32[]{:S(2)}) copy-start(f32[2,4,256,256]{3,2,1,0:T(8,128)} %far_cross.3) | copy-start | bytes 6291460
  102.4 1.6 copy-start.1
  106.5 31.5 %copy-start.6 = (f32[2,8,256]{2,1,0:T(8,128)S(1)}, f32[2,8,256]{2,1,0:T(8,128)}, u32[]{:S(2)}) copy-start(f32[2,8,256]{2,1,0:T(8,128)} %solution_ref.1) | copy-start | bytes 49156
  134.8 3.2 %collective-permute-start.7 = (f32[64,5,8,128]{3,2,1,0:T(8,128)S(1)}, f32[64,5,8,128]{3,2,1,0:T(8,128)}, u32[]{:S(2)}, u32[]{:S(2)}) collective-permute-start(f32[64,5,8,128]{3,2,1,0:T(8,128)S(1)} %all_to_all.16.mine_ref), channel_id=1, source_target_pairs={{0,1},{1,0},{2,3},{3,2},{4,5},{5,4},{6,7},{7,6},{8,9},{9,8},{10,11... | collective-permute-start | bytes 3932168 | tf_op jit(solution)/shard_map/ppermute | solution.py:450
  138.0 1.0 copy-start.3
  144.7 3.1 %collective-permute-start.8 = (f32[64,5,8,128]{3,2,1,0:T(8,128)S(1)}, f32[64,5,8,128]{3,2,1,0:T(8,128)S(1)}, u32[]{:S(2)}, u32[]{:S(2)}) collective-permute-start(f32[64,5,8,128]{3,2,1,0:T(8,128)S(1)} %slice.7), channel_id=1, source_target_pairs={{0,1},{1,0},{2,3},{3,2},{4,5},{5,4},{6,7},{7,6},{8,9},{9,8},{10,11... | collective-permute-start | bytes 3932168 | tf_op jit(solution)/shard_map/ppermute | solution.py:450
Sparse Core Ops, SparseCore 0:
  11.2 73.1 all-gather.1

commit v5 on v4

--- a/solution.py
+++ b/solution.py
@@ -17,7 +17,7 @@
 AXES = ("row", "col")
 BS, RHS, NBR, OWN = 256, 8, 4, 2
 HALF = 128
-STEP = 4
+STEP = 8
 PEERS = 64
 GUARD = 2.0**-20
 PAIR = 2 * OWN * BS

time: 183 us -> 178 us (0.973)
  Pallas kernels: 76.9 us -> 71 us
    pallas_call x3, Pallas kernels: 63.4 us -> 57.5 us  [add_image(): pl.pallas_call(functools.partial(image_kernel, pieces), grid=(pieces * ea...]
  transfers between devices with their start and end apart: 10 -> 10, of which waited for: 3 -> 4; matrix products, arithmetic and copies ran while one was open for 0% -> 0% of each run, Pallas kernels for 37% -> 35%
where the time goes in v5:
time: 178 us; the launch traced here: 177 us
  blocking collectives  72.6 us (41%)
  Pallas kernels  71 us (40%)
  between operations  14.3 us (8%)
  waiting for transfers between devices  9.15 us (5%)
  starting transfers between devices  5.9 us (3%)
  local copies, waits for them, and re-layouts  3.85 us (2%)
    all_to_all x3, blocking collectives, exchange(): lax.all_to_all(value, AXES, 0, 0, axis_index_groups=groups, tiled=True)  72.6 us
    pallas_call x3, Pallas kernels, add_image(): pl.pallas_call(functools.partial(image_kernel, pieces), grid=(pieces * ea...  57.5 us
    ppermute x6, waiting for transfers between devices, to_other_core(): return lax.ppermute(value, 'col', [(i, i ^ 1) for i in range(32)])  7.3 us
    pallas_call x1, Pallas kernels, spread_step(): pl.pallas_call(spread_kernel, out_shape=(own, own, own, jax.ShapeDtypeStr...  5.56 us
    ppermute x3, starting transfers between devices, per_device(): beyond = [x_around(hop)(plane) for hop in (1, 3, 2)]  5.05 us
    pallas_call x1, Pallas kernels, point_payload(): pl.pallas_call(pick_points, out_shape=(jax.ShapeDtypeStruct((copies, 6, R...  4.7 us
  transfers between devices with their start and end apart: 10, of which 4 were waited for; matrix products, arithmetic and copies ran while one was open for 0% of the time, Pallas kernels for 35%

profile of v5, /device:TPU:0, one launch (start us, length us, event | category | flops | bytes accessed | tf_op | source)
XLA Modules:
  0.0 177.0 jit_solution(4434421005022344109)
XLA Ops:
  7.2 0.7 all-gather.2.cloned.1.call-update
  7.9 4.7 %pick_points.1 = (f32[16,6,8,128]{3,2,1,0:T(8,128)}, f32[6,8,128]{2,1,0:T(8,128)}) custom-call(s32[65536]{0:T(1024)} %all_order.1, f32[3,65536]{1,0:T(4,128)} %all_coordinates.1, f32[2,8,256]{2,1,0:T(8,128)} %direction_ref.7), custom_call_target="tpu_custom_call" | custom-call | tf_op jit(solution)/shard_map/pick_points/pallas_call | solution.py:108
  12.6 18.0 %all_to_all.15.refs_0_ = f32[16,6,8,128]{3,2,1,0:T(8,128)S(1)} all-to-all(f32[16,6,8,128]{3,2,1,0:T(8,128)} %get-tuple-element.15), channel_id=1, replica_groups={{0,2,4,6,32,34,36,38,64,66,68,70,96,98,100,102},{1,3,5,7,33,35,37,39,65..., dimensions={0} | all-to-all | bytes 786432 | tf_op jit(solution)/shard_map/all_to_all | solution.py:454
  31.0 1.3 collective-permute-done.refs_1_
  32.3 3.0 %collective-permute-start.3 = (f32[16,6,8,128]{3,2,1,0:T(8,128)S(1)}, f32[16,6,8,128]{3,2,1,0:T(8,128)S(1)}, u32[]{:S(2)}, u32[]{:S(2)}) collective-permute-start(f32[16,6,8,128]{3,2,1,0:T(8,128)S(1)} %all_to_all.15.refs_0_), channel_id=1, source_target_pairs={{0,16},{1,17},{2,18},{3,19},{4,20},{5,21},{6,22},{7,23},{8,24},{9,... | collective-permute-start | bytes 1179656 | tf_op jit(solution)/shard_map/ppermute | solution.py:485
  35.3 1.1 collective-permute-start.2
  36.5 0.9 collective-permute-start.1
  37.4 0.7 copy-done.7
  38.1 14.4 %image.3.start_ref = f32[16,512]{1,0:T(8,128)S(1)} custom-call(f32[6,8,128]{2,1,0:T(8,128)S(1)} %copy-done.7, f32[16,512]{1,0:T(8,128)S(1)} %broadcast_in_dim.8.start_ref, f32[16,6,8,128]{3,2,1,0:T(8,128)S(1)} %all_to_all.15.refs_0_, f32[16,6,8,128]{3,2,1,0:T(8,128)S(1)} %collective-permute-done.refs_1_), custom_call_target="tpu_custom_call" | custom-call | flops 5033164800 | bytes 786432 | tf_op jit(solution)/shard_map/image/pallas_call | solution.py:196
  52.6 1.1 collective-permute-done.2.refs_1_
  53.7 0.5 collective-permute-start.4
  54.3 21.6 %image.4.start_ref = f32[16,512]{1,0:T(8,128)S(1)} custom-call(f32[6,8,128]{2,1,0:T(8,128)S(1)} %copy-done.7, f32[16,512]{1,0:T(8,128)S(1)} %image.3.start_ref, f32[16,6,8,128]{3,2,1,0:T(8,128)S(1)} %collective-permute-done.1.refs_0_, f32[16,6,8,128]{3,2,1,0:T(8,128)S(1)} %collective-permute-done.2.refs_1_, f32[16,6,8,128]{3,2,1,0:T(8,128)S(1)} %collective-permute-done.3.refs_2_), custom_call_target="tpu_custom_call" | custom-call | flops 7549747200 | bytes 1179648 | tf_op jit(solution)/shard_map/image/pallas_call | solution.py:196
  75.9 21.5 %image.5.sum_ref = f32[16,512]{1,0:T(8,128)S(1)} custom-call(f32[6,8,128]{2,1,0:T(8,128)S(1)} %copy-done.8, f32[16,512]{1,0:T(8,128)S(1)} %image.4.start_ref, f32[16,6,8,128]{3,2,1,0:T(8,128)S(1)} %collective-permute-done.4.refs_0_, f32[16,6,8,128]{3,2,1,0:T(8,128)S(1)} %collective-permute-done.5.refs_1_, f32[16,6,8,128]{3,2,1,0:T(8,128)S(1)} %collective-permute-done.6.refs_2_), custom_call_target="tpu_custom_call" | custom-call | flops 7549747200 | bytes 1179648 | tf_op jit(solution)/shard_map/image/pallas_call | solution.py:196
  97.6 1.6 copy-done.1
  99.2 2.5 %measure_step.1 = (f32[64,5,8,128]{3,2,1,0:T(8,128)S(1)}, f32[8,8,256]{2,1,0:T(8,128)S(1)}) custom-call(s32[8]{0:T(128)S(1)} %reshape.18.list_ref, s32[8]{0:T(128)S(1)} %reshape.22.valid_ref, f32[256,8,256]{2,1,0:T(8,128)S(1)} %copy-done.1, f32[2,8,256]{2,1,0:T(8,128)S(1)} %copy-done.5, f32[2,4,256,256]{3,2,1,0:T(8,128)S(1)} %copy-done, ...), custom_call_target="tpu_custom_call" | custom-call | tf_op jit(solution)/shard_map/measure_step/pallas_call | solution.py:301
  101.7 28.2 %all_to_all.16.mine_ref = f32[64,5,8,128]{3,2,1,0:T(8,128)S(1)} all-to-all(f32[64,5,8,128]{3,2,1,0:T(8,128)S(1)} %get-tuple-element.18), channel_id=1, replica_groups={{0,2,4,6,8,10,12,14,16,18,20,22,24,26,28,30,32,34,36,38,40,42,44,46,48,..., dimensions={0} | all-to-all | bytes 2621440 | tf_op jit(solution)/shard_map/all_to_all | solution.py:454
  129.9 3.1 %collective-permute-done.7.other_ref = f32[64,5,8,128]{3,2,1,0:T(8,128)} collective-permute-done((f32[64,5,8,128]{3,2,1,0:T(8,128)S(1)}, f32[64,5,8,128]{3,2,1,0:T(8,128)}, u32[]{:S(2)}, u32[]{:S(2)}) %collective-permute-start.7) | collective-permute-done | bytes 1310752 | tf_op jit(solution)/shard_map/ppermute | solution.py:450
  133.0 1.0 copy-done.3
  134.0 5.6 %spread_step.1 = (f32[2,8,256]{2,1,0:T(8,128)}, f32[2,8,256]{2,1,0:T(8,128)}, f32[2,8,256]{2,1,0:T(8,128)S(1)}, f32[128,5,8,128]{3,2,1,0:T(8,128)S(1)}, f32[8,128]{1,0:T(8,128)S(1)}) custom-call(s32[8]{0:T(128)S(1)} %multiply_add_fusion.1.at_ref, s32[8]{0:T(128)S(1)} %reshape.22.valid_ref, s32[8]{0:T(128)S(1)} %get-tuple-element.25.into_ref, ...), custom_call_target="tpu_custom_call" | custom-call | tf_op jit(solution)/shard_map/spread_step/pallas_call | solution.py:415
  139.7 0.2 collective-permute-start.8
  139.9 2.9 %collective-permute-done.8 = f32[64,5,8,128]{3,2,1,0:T(8,128)S(1)} collective-permute-done((f32[64,5,8,128]{3,2,1,0:T(8,128)S(1)}, f32[64,5,8,128]{3,2,1,0:T(8,128)S(1)}, u32[]{:S(2)}, u32[]{:S(2)}) %collective-permute-start.8) | collective-permute-done | bytes 1310752 | tf_op jit(solution)/shard_map/ppermute | solution.py:450
  142.8 0.1 slice_add_fusion
  143.0 26.5 %all_to_all.17.all_ref = f32[64,5,8,128]{3,2,1,0:T(8,128)S(1)} all-to-all(f32[64,5,8,128]{3,2,1,0:T(8,128)S(1)} %slice_add_fusion), channel_id=1, replica_groups={{0,2,4,6,8,10,12,14,16,18,20,22,24,26,28,30,32,34,36,38,40,42,44,46,48,..., dimensions={0} | all-to-all | bytes 2621440 | tf_op jit(solution)/shard_map/all_to_all | solution.py:454
  169.4 0.7 sum_step.1
  (39 shorter events, 0.8 us)
Async XLA Ops:
  7.2 23.4 %copy-start.9 = (s32[256,4]{0,1:T(4,128)S(1)}, s32[256,4]{0,1:T(4,128)}, u32[]{:S(2)}) copy-start(s32[256,4]{0,1:T(4,128)} %param.10) | copy-start | bytes 12292
  7.2 90.3 %all-gather.2.cloned.1.call-start = ((), (), s32[]{:S(2)}) async-start(), calls=%async_computation.3 | async-start | bytes 2113536 | tf_op jit(solution)/shard_map/all_gather | solution.py:480
  30.6 1.7 collective-permute-start
  32.3 20.2 %collective-permute-start.3 = (f32[16,6,8,128]{3,2,1,0:T(8,128)S(1)}, f32[16,6,8,128]{3,2,1,0:T(8,128)S(1)}, u32[]{:S(2)}, u32[]{:S(2)}) collective-permute-start(f32[16,6,8,128]{3,2,1,0:T(8,128)S(1)} %all_to_all.15.refs_0_), channel_id=1, source_target_pairs={{0,16},{1,17},{2,18},{3,19},{4,20},{5,21},{6,22},{7,23},{8,24},{9,... | collective-permute-start | bytes 1179656 | tf_op jit(solution)/shard_map/ppermute | solution.py:485
  35.3 18.4 %collective-permute-start.2 = (f32[16,6,8,128]{3,2,1,0:T(8,128)S(1)}, f32[16,6,8,128]{3,2,1,0:T(8,128)S(1)}, u32[]{:S(2)}, u32[]{:S(2)}) collective-permute-start(f32[16,6,8,128]{3,2,1,0:T(8,128)S(1)} %all_to_all.15.refs_0_), channel_id=1, source_target_pairs={{0,24},{1,25},{2,26},{3,27},{4,28},{5,29},{6,30},{7,31},{8,0},{9,1... | collective-permute-start | bytes 1179656 | tf_op jit(solution)/shard_map/ppermute | solution.py:485
  36.5 17.3 %collective-permute-start.1 = (f32[16,6,8,128]{3,2,1,0:T(8,128)S(1)}, f32[16,6,8,128]{3,2,1,0:T(8,128)S(1)}, u32[]{:S(2)}, u32[]{:S(2)}) collective-permute-start(f32[16,6,8,128]{3,2,1,0:T(8,128)S(1)} %all_to_all.15.refs_0_), channel_id=1, source_target_pairs={{0,8},{1,9},{2,10},{3,11},{4,12},{5,13},{6,14},{7,15},{8,16},{9,17... | collective-permute-start | bytes 1179656 | tf_op jit(solution)/shard_map/ppermute | solution.py:485
  37.4 0.7 copy-start.7
  52.5 23.4 %copy-start.8 = (f32[6,8,128]{2,1,0:T(8,128)S(1)}, f32[6,8,128]{2,1,0:T(8,128)}, u32[]{:S(2)}) copy-start(f32[6,8,128]{2,1,0:T(8,128)} %get-tuple-element.14.own_ref) | copy-start | bytes 73732
  52.5 23.4 %collective-permute-start.6 = (f32[16,6,8,128]{3,2,1,0:T(8,128)S(1)}, f32[16,6,8,128]{3,2,1,0:T(8,128)S(1)}, u32[]{:S(2)}, u32[]{:S(2)}) collective-permute-start(f32[16,6,8,128]{3,2,1,0:T(8,128)S(1)} %collective-permute-done.3.refs_2_), channel_id=1, source_target_pairs={{0,1},{1,0},{2,3},{3,2},{4,5},{5,4},{6,7},{7,6},{8,9},{9,8},{10,11... | collective-permute-start | bytes 1179656 | tf_op jit(solution)/shard_map/ppermute | solution.py:450
  53.7 22.2 %collective-permute-start.5 = (f32[16,6,8,128]{3,2,1,0:T(8,128)S(1)}, f32[16,6,8,128]{3,2,1,0:T(8,128)S(1)}, u32[]{:S(2)}, u32[]{:S(2)}) collective-permute-start(f32[16,6,8,128]{3,2,1,0:T(8,128)S(1)} %collective-permute-done.2.refs_1_), channel_id=1, source_target_pairs={{0,1},{1,0},{2,3},{3,2},{4,5},{5,4},{6,7},{7,6},{8,9},{9,8},{10,11... | collective-permute-start | bytes 1179656 | tf_op jit(solution)/shard_map/ppermute | solution.py:450
  53.7 22.2 %collective-permute-start.4 = (f32[16,6,8,128]{3,2,1,0:T(8,128)S(1)}, f32[16,6,8,128]{3,2,1,0:T(8,128)S(1)}, u32[]{:S(2)}, u32[]{:S(2)}) collective-permute-start(f32[16,6,8,128]{3,2,1,0:T(8,128)S(1)} %collective-permute-done.1.refs_0_), channel_id=1, source_target_pairs={{0,1},{1,0},{2,3},{3,2},{4,5},{5,4},{6,7},{7,6},{8,9},{9,8},{10,11... | collective-permute-start | bytes 1179656 | tf_op jit(solution)/shard_map/ppermute | solution.py:450
  75.9 21.7 %copy-start.2 = (f32[2,256,256]{2,1,0:T(8,128)S(1)}, f32[2,256,256]{2,1,0:T(8,128)}, u32[]{:S(2)}) copy-start(f32[2,256,256]{2,1,0:T(8,128)} %far_whitening.3) | copy-start | bytes 1572868
  75.9 21.7 %copy-start.4 = (f32[2,8,256]{2,1,0:T(8,128)S(1)}, f32[2,8,256]{2,1,0:T(8,128)}, u32[]{:S(2)}) copy-start(f32[2,8,256]{2,1,0:T(8,128)} %direction_ref.7) | copy-start | bytes 49156
  75.9 21.7 %copy-start.5 = (f32[2,8,256]{2,1,0:T(8,128)S(1)}, f32[2,8,256]{2,1,0:T(8,128)}, u32[]{:S(2)}) copy-start(f32[2,8,256]{2,1,0:T(8,128)} %residual_ref.3) | copy-start | bytes 49156
  75.9 21.6 %copy-start = (f32[2,4,256,256]{3,2,1,0:T(8,128)S(1)}, f32[2,4,256,256]{3,2,1,0:T(8,128)}, u32[]{:S(2)}) copy-start(f32[2,4,256,256]{3,2,1,0:T(8,128)} %far_cross.3) | copy-start | bytes 6291460
  97.6 1.6 copy-start.1
  101.6 31.3 %copy-start.6 = (f32[2,8,256]{2,1,0:T(8,128)S(1)}, f32[2,8,256]{2,1,0:T(8,128)}, u32[]{:S(2)}) copy-start(f32[2,8,256]{2,1,0:T(8,128)} %solution_ref.1) | copy-start | bytes 49156
  129.8 3.2 %collective-permute-start.7 = (f32[64,5,8,128]{3,2,1,0:T(8,128)S(1)}, f32[64,5,8,128]{3,2,1,0:T(8,128)}, u32[]{:S(2)}, u32[]{:S(2)}) collective-permute-start(f32[64,5,8,128]{3,2,1,0:T(8,128)S(1)} %all_to_all.16.mine_ref), channel_id=1, source_target_pairs={{0,1},{1,0},{2,3},{3,2},{4,5},{5,4},{6,7},{7,6},{8,9},{9,8},{10,11... | collective-permute-start | bytes 3932168 | tf_op jit(solution)/shard_map/ppermute | solution.py:450
  133.0 1.0 copy-start.3
  139.7 3.1 %collective-permute-start.8 = (f32[64,5,8,128]{3,2,1,0:T(8,128)S(1)}, f32[64,5,8,128]{3,2,1,0:T(8,128)S(1)}, u32[]{:S(2)}, u32[]{:S(2)}) collective-permute-start(f32[64,5,8,128]{3,2,1,0:T(8,128)S(1)} %slice.7), channel_id=1, source_target_pairs={{0,1},{1,0},{2,3},{3,2},{4,5},{5,4},{6,7},{7,6},{8,9},{9,8},{10,11... | collective-permute-start | bytes 3932168 | tf_op jit(solution)/shard_map/ppermute | solution.py:450
Sparse Core Ops, SparseCore 0:
  11.2 73.1 all-gather.1

commit v6 on v5

--- a/solution.py
+++ b/solution.py
@@ -17,7 +17,6 @@
 AXES = ("row", "col")
 BS, RHS, NBR, OWN = 256, 8, 4, 2
 HALF = 128
-STEP = 8
 PEERS = 64
 GUARD = 2.0**-20
 PAIR = 2 * OWN * BS
@@ -133,6 +132,7 @@
 def image_kernel(pieces, own_ref, start_ref, *refs):
     columns, (out_ref, own_part, column_part, field_part, square) = refs[:pieces], refs[pieces:]
     each = pl.num_programs(0) // pieces
+    step = columns[0].shape[0]
 
     @pl.when(pl.program_id(0) == 0)
     def _():
@@ -141,7 +141,7 @@
         out_ref[...] = start_ref[...]
 
     def prepare(columns_ref):
-        for member in range(STEP):
+        for member in range(step):
             for block in range(OWN):
                 at = OWN * member + block
                 tiles = columns_ref.at[member]
@@ -152,7 +152,7 @@
     for index, columns_ref in enumerate(columns):
         pl.when(pl.program_id(0) // each == index)(functools.partial(prepare, columns_ref))
     jobs = [
-        (q, r) for r in range(OWN * BS // WIDE) for q in range(STEP * OWN * BS // TALL)
+        (q, r) for r in range(OWN * BS // WIDE) for q in range(step * OWN * BS // TALL)
     ]
 
     def fill(job, slot):
@@ -182,14 +182,14 @@
                 ) + jnp.dot(field, low, preferred_element_type=f32)
 
 
-def add_image(own, columns, start):
+def add_image(own, columns, start, step):
     pieces, count = len(columns), columns[0].shape[0]
-    each = count // STEP
+    each = count // step
     pairs = pieces * count * OWN * BS * OWN * BS
 
     def piece_spec(index):
         return pl.BlockSpec(
-            (STEP, 6, RHS, HALF),
+            (step, 6, RHS, HALF),
             lambda i: (jnp.clip(i - index * each, 0, each - 1), 0, 0, 0),
         )
 
@@ -205,8 +205,8 @@
         out_shape=jax.ShapeDtypeStruct((2 * RHS, OWN * BS), f32),
         scratch_shapes=[
             pltpu.VMEM((48, OWN * BS), bf16),
-            pltpu.VMEM((STEP * OWN * BS, 48), bf16),
-            pltpu.VMEM((OWN * STEP, 2 * RHS, BS), bf16),
+            pltpu.VMEM((step * OWN * BS, 48), bf16),
+            pltpu.VMEM((OWN * step, 2 * RHS, BS), bf16),
             pltpu.VMEM((2, TALL, WIDE), f32),
         ],
         compiler_params=pltpu.CompilerParams(vmem_limit_bytes=10 * MEGA),
@@ -483,10 +483,10 @@
     plane = exchange(payload, SAME_X_CORE)
     plane, plane_other = lax.optimization_barrier((plane, to_other_core(plane)))
     beyond = [x_around(hop)(plane) for hop in (1, 3, 2)]
-    total = add_image(own, [plane, plane_other], jnp.zeros((2 * RHS, OWN * BS), f32))
+    total = add_image(own, [plane, plane_other], jnp.zeros((2 * RHS, OWN * BS), f32), 8)
     others = [to_other_core(piece) for piece in beyond]
-    total = add_image(own, beyond, total)
-    total = add_image(own, others, total)
+    total = add_image(own, beyond, total, 16)
+    total = add_image(own, others, total, 16)
 
     image, near = measure_step(
         lists, valid, gathered, residual, cross, whitening, total, direction

time: 178 us -> 176 us (0.989)
  no operation moved by 1% of the time
where the time goes in v6:
time: 176 us; the launch traced here: 175 us
  blocking collectives  72.6 us (41%)
  Pallas kernels  69.4 us (39%)
  between operations  14.3 us (8%)
  waiting for transfers between devices  9.15 us (5%)
  starting transfers between devices  5.9 us (3%)
  local copies, waits for them, and re-layouts  3.85 us (2%)
    all_to_all x3, blocking collectives, exchange(): lax.all_to_all(value, AXES, 0, 0, axis_index_groups=groups, tiled=True)  72.6 us
    pallas_call x3, Pallas kernels, add_image(): pl.pallas_call(functools.partial(image_kernel, pieces), grid=(pieces * ea...  56 us
    ppermute x6, waiting for transfers between devices, to_other_core(): return lax.ppermute(value, 'col', [(i, i ^ 1) for i in range(32)])  7.29 us
    pallas_call x1, Pallas kernels, spread_step(): pl.pallas_call(spread_kernel, out_shape=(own, own, own, jax.ShapeDtypeStr...  5.56 us
    ppermute x3, starting transfers between devices, per_device(): beyond = [x_around(hop)(plane) for hop in (1, 3, 2)]  5.05 us
    pallas_call x1, Pallas kernels, point_payload(): pl.pallas_call(pick_points, out_shape=(jax.ShapeDtypeStruct((copies, 6, R...  4.7 us
  transfers between devices with their start and end apart: 10, of which 4 were waited for; matrix products, arithmetic and copies ran while one was open for 0% of the time, Pallas kernels for 35%

profile of v6, /device:TPU:0, one launch (start us, length us, event | category | flops | bytes accessed | tf_op | source)
XLA Modules:
  0.0 175.4 jit_solution(3618807411976633074)
XLA Ops:
  7.2 0.7 all-gather.2.cloned.1.call-update
  7.9 4.7 %pick_points.1 = (f32[16,6,8,128]{3,2,1,0:T(8,128)}, f32[6,8,128]{2,1,0:T(8,128)}) custom-call(s32[65536]{0:T(1024)} %all_order.1, f32[3,65536]{1,0:T(4,128)} %all_coordinates.1, f32[2,8,256]{2,1,0:T(8,128)} %direction_ref.7), custom_call_target="tpu_custom_call" | custom-call | tf_op jit(solution)/shard_map/pick_points/pallas_call | solution.py:107
  12.6 18.0 %all_to_all.15.refs_0_ = f32[16,6,8,128]{3,2,1,0:T(8,128)S(1)} all-to-all(f32[16,6,8,128]{3,2,1,0:T(8,128)} %get-tuple-element.15), channel_id=1, replica_groups={{0,2,4,6,32,34,36,38,64,66,68,70,96,98,100,102},{1,3,5,7,33,35,37,39,65..., dimensions={0} | all-to-all | bytes 786432 | tf_op jit(solution)/shard_map/all_to_all | solution.py:454
  31.0 1.3 collective-permute-done.refs_1_
  32.3 3.0 %collective-permute-start.3 = (f32[16,6,8,128]{3,2,1,0:T(8,128)S(1)}, f32[16,6,8,128]{3,2,1,0:T(8,128)S(1)}, u32[]{:S(2)}, u32[]{:S(2)}) collective-permute-start(f32[16,6,8,128]{3,2,1,0:T(8,128)S(1)} %all_to_all.15.refs_0_), channel_id=1, source_target_pairs={{0,16},{1,17},{2,18},{3,19},{4,20},{5,21},{6,22},{7,23},{8,24},{9,... | collective-permute-start | bytes 1179656 | tf_op jit(solution)/shard_map/ppermute | solution.py:485
  35.3 1.1 collective-permute-start.2
  36.5 0.9 collective-permute-start.1
  37.4 0.7 copy-done.7
  38.1 14.4 %image.3.start_ref = f32[16,512]{1,0:T(8,128)S(1)} custom-call(f32[6,8,128]{2,1,0:T(8,128)S(1)} %copy-done.7, f32[16,512]{1,0:T(8,128)S(1)} %broadcast_in_dim.8.start_ref, f32[16,6,8,128]{3,2,1,0:T(8,128)S(1)} %all_to_all.15.refs_0_, f32[16,6,8,128]{3,2,1,0:T(8,128)S(1)} %collective-permute-done.refs_1_), custom_call_target="tpu_custom_call" | custom-call | flops 5033164800 | bytes 786432 | tf_op jit(solution)/shard_map/image/pallas_call | solution.py:196
  52.6 1.1 collective-permute-done.2.refs_1_
  53.7 0.5 collective-permute-start.4
  54.3 20.7 %image.4.start_ref = f32[16,512]{1,0:T(8,128)S(1)} custom-call(f32[6,8,128]{2,1,0:T(8,128)S(1)} %copy-done.7, f32[16,512]{1,0:T(8,128)S(1)} %image.3.start_ref, f32[16,6,8,128]{3,2,1,0:T(8,128)S(1)} %collective-permute-done.1.refs_0_, f32[16,6,8,128]{3,2,1,0:T(8,128)S(1)} %collective-permute-done.2.refs_1_, f32[16,6,8,128]{3,2,1,0:T(8,128)S(1)} %collective-permute-done.3.refs_2_), custom_call_target="tpu_custom_call" | custom-call | flops 7549747200 | bytes 1179648 | tf_op jit(solution)/shard_map/image/pallas_call | solution.py:196
  75.1 20.9 %image.5.sum_ref = f32[16,512]{1,0:T(8,128)S(1)} custom-call(f32[6,8,128]{2,1,0:T(8,128)S(1)} %copy-done.8, f32[16,512]{1,0:T(8,128)S(1)} %image.4.start_ref, f32[16,6,8,128]{3,2,1,0:T(8,128)S(1)} %collective-permute-done.4.refs_0_, f32[16,6,8,128]{3,2,1,0:T(8,128)S(1)} %collective-permute-done.5.refs_1_, f32[16,6,8,128]{3,2,1,0:T(8,128)S(1)} %collective-permute-done.6.refs_2_), custom_call_target="tpu_custom_call" | custom-call | flops 7549747200 | bytes 1179648 | tf_op jit(solution)/shard_map/image/pallas_call | solution.py:196
  96.0 1.6 copy-done.1
  97.6 2.5 %measure_step.1 = (f32[64,5,8,128]{3,2,1,0:T(8,128)S(1)}, f32[8,8,256]{2,1,0:T(8,128)S(1)}) custom-call(s32[8]{0:T(128)S(1)} %reshape.18.list_ref, s32[8]{0:T(128)S(1)} %reshape.22.valid_ref, f32[256,8,256]{2,1,0:T(8,128)S(1)} %copy-done.1, f32[2,8,256]{2,1,0:T(8,128)S(1)} %copy-done.5, f32[2,4,256,256]{3,2,1,0:T(8,128)S(1)} %copy-done, ...), custom_call_target="tpu_custom_call" | custom-call | tf_op jit(solution)/shard_map/measure_step/pallas_call | solution.py:301
  100.1 28.2 %all_to_all.16.mine_ref = f32[64,5,8,128]{3,2,1,0:T(8,128)S(1)} all-to-all(f32[64,5,8,128]{3,2,1,0:T(8,128)S(1)} %get-tuple-element.18), channel_id=1, replica_groups={{0,2,4,6,8,10,12,14,16,18,20,22,24,26,28,30,32,34,36,38,40,42,44,46,48,..., dimensions={0} | all-to-all | bytes 2621440 | tf_op jit(solution)/shard_map/all_to_all | solution.py:454
  128.3 3.1 %collective-permute-done.7.other_ref = f32[64,5,8,128]{3,2,1,0:T(8,128)} collective-permute-done((f32[64,5,8,128]{3,2,1,0:T(8,128)S(1)}, f32[64,5,8,128]{3,2,1,0:T(8,128)}, u32[]{:S(2)}, u32[]{:S(2)}) %collective-permute-start.7) | collective-permute-done | bytes 1310752 | tf_op jit(solution)/shard_map/ppermute | solution.py:450
  131.4 1.0 copy-done.3
  132.5 5.6 %spread_step.1 = (f32[2,8,256]{2,1,0:T(8,128)}, f32[2,8,256]{2,1,0:T(8,128)}, f32[2,8,256]{2,1,0:T(8,128)S(1)}, f32[128,5,8,128]{3,2,1,0:T(8,128)S(1)}, f32[8,128]{1,0:T(8,128)S(1)}) custom-call(s32[8]{0:T(128)S(1)} %multiply_add_fusion.1.at_ref, s32[8]{0:T(128)S(1)} %reshape.22.valid_ref, s32[8]{0:T(128)S(1)} %get-tuple-element.25.into_ref, ...), custom_call_target="tpu_custom_call" | custom-call | tf_op jit(solution)/shard_map/spread_step/pallas_call | solution.py:415
  138.1 0.2 collective-permute-start.8
  138.4 2.9 %collective-permute-done.8 = f32[64,5,8,128]{3,2,1,0:T(8,128)S(1)} collective-permute-done((f32[64,5,8,128]{3,2,1,0:T(8,128)S(1)}, f32[64,5,8,128]{3,2,1,0:T(8,128)S(1)}, u32[]{:S(2)}, u32[]{:S(2)}) %collective-permute-start.8) | collective-permute-done | bytes 1310752 | tf_op jit(solution)/shard_map/ppermute | solution.py:450
  141.3 0.1 slice_add_fusion
  141.4 26.5 %all_to_all.17.all_ref = f32[64,5,8,128]{3,2,1,0:T(8,128)S(1)} all-to-all(f32[64,5,8,128]{3,2,1,0:T(8,128)S(1)} %slice_add_fusion), channel_id=1, replica_groups={{0,2,4,6,8,10,12,14,16,18,20,22,24,26,28,30,32,34,36,38,40,42,44,46,48,..., dimensions={0} | all-to-all | bytes 2621440 | tf_op jit(solution)/shard_map/all_to_all | solution.py:454
  167.9 0.7 sum_step.1
  (39 shorter events, 0.8 us)
Async XLA Ops:
  7.2 23.4 %copy-start.9 = (s32[256,4]{0,1:T(4,128)S(1)}, s32[256,4]{0,1:T(4,128)}, u32[]{:S(2)}) copy-start(s32[256,4]{0,1:T(4,128)} %param.10) | copy-start | bytes 12292
  7.2 88.8 %all-gather.2.cloned.1.call-start = ((), (), s32[]{:S(2)}) async-start(), calls=%async_computation.3 | async-start | bytes 2113536 | tf_op jit(solution)/shard_map/all_gather | solution.py:480
  30.6 1.7 collective-permute-start
  32.3 20.2 %collective-permute-start.3 = (f32[16,6,8,128]{3,2,1,0:T(8,128)S(1)}, f32[16,6,8,128]{3,2,1,0:T(8,128)S(1)}, u32[]{:S(2)}, u32[]{:S(2)}) collective-permute-start(f32[16,6,8,128]{3,2,1,0:T(8,128)S(1)} %all_to_all.15.refs_0_), channel_id=1, source_target_pairs={{0,16},{1,17},{2,18},{3,19},{4,20},{5,21},{6,22},{7,23},{8,24},{9,... | collective-permute-start | bytes 1179656 | tf_op jit(solution)/shard_map/ppermute | solution.py:485
  35.3 18.4 %collective-permute-start.2 = (f32[16,6,8,128]{3,2,1,0:T(8,128)S(1)}, f32[16,6,8,128]{3,2,1,0:T(8,128)S(1)}, u32[]{:S(2)}, u32[]{:S(2)}) collective-permute-start(f32[16,6,8,128]{3,2,1,0:T(8,128)S(1)} %all_to_all.15.refs_0_), channel_id=1, source_target_pairs={{0,24},{1,25},{2,26},{3,27},{4,28},{5,29},{6,30},{7,31},{8,0},{9,1... | collective-permute-start | bytes 1179656 | tf_op jit(solution)/shard_map/ppermute | solution.py:485
  36.5 17.3 %collective-permute-start.1 = (f32[16,6,8,128]{3,2,1,0:T(8,128)S(1)}, f32[16,6,8,128]{3,2,1,0:T(8,128)S(1)}, u32[]{:S(2)}, u32[]{:S(2)}) collective-permute-start(f32[16,6,8,128]{3,2,1,0:T(8,128)S(1)} %all_to_all.15.refs_0_), channel_id=1, source_target_pairs={{0,8},{1,9},{2,10},{3,11},{4,12},{5,13},{6,14},{7,15},{8,16},{9,17... | collective-permute-start | bytes 1179656 | tf_op jit(solution)/shard_map/ppermute | solution.py:485
  37.4 0.7 copy-start.7
  52.5 22.6 %copy-start.8 = (f32[6,8,128]{2,1,0:T(8,128)S(1)}, f32[6,8,128]{2,1,0:T(8,128)}, u32[]{:S(2)}) copy-start(f32[6,8,128]{2,1,0:T(8,128)} %get-tuple-element.14.own_ref) | copy-start | bytes 73732
  52.5 22.5 %collective-permute-start.6 = (f32[16,6,8,128]{3,2,1,0:T(8,128)S(1)}, f32[16,6,8,128]{3,2,1,0:T(8,128)S(1)}, u32[]{:S(2)}, u32[]{:S(2)}) collective-permute-start(f32[16,6,8,128]{3,2,1,0:T(8,128)S(1)} %collective-permute-done.3.refs_2_), channel_id=1, source_target_pairs={{0,1},{1,0},{2,3},{3,2},{4,5},{5,4},{6,7},{7,6},{8,9},{9,8},{10,11... | collective-permute-start | bytes 1179656 | tf_op jit(solution)/shard_map/ppermute | solution.py:450
  53.7 21.3 %collective-permute-start.5 = (f32[16,6,8,128]{3,2,1,0:T(8,128)S(1)}, f32[16,6,8,128]{3,2,1,0:T(8,128)S(1)}, u32[]{:S(2)}, u32[]{:S(2)}) collective-permute-start(f32[16,6,8,128]{3,2,1,0:T(8,128)S(1)} %collective-permute-done.2.refs_1_), channel_id=1, source_target_pairs={{0,1},{1,0},{2,3},{3,2},{4,5},{5,4},{6,7},{7,6},{8,9},{9,8},{10,11... | collective-permute-start | bytes 1179656 | tf_op jit(solution)/shard_map/ppermute | solution.py:450
  53.7 21.3 %collective-permute-start.4 = (f32[16,6,8,128]{3,2,1,0:T(8,128)S(1)}, f32[16,6,8,128]{3,2,1,0:T(8,128)S(1)}, u32[]{:S(2)}, u32[]{:S(2)}) collective-permute-start(f32[16,6,8,128]{3,2,1,0:T(8,128)S(1)} %collective-permute-done.1.refs_0_), channel_id=1, source_target_pairs={{0,1},{1,0},{2,3},{3,2},{4,5},{5,4},{6,7},{7,6},{8,9},{9,8},{10,11... | collective-permute-start | bytes 1179656 | tf_op jit(solution)/shard_map/ppermute | solution.py:450
  75.0 21.0 %copy-start.2 = (f32[2,256,256]{2,1,0:T(8,128)S(1)}, f32[2,256,256]{2,1,0:T(8,128)}, u32[]{:S(2)}) copy-start(f32[2,256,256]{2,1,0:T(8,128)} %far_whitening.3) | copy-start | bytes 1572868
  75.0 21.0 %copy-start.4 = (f32[2,8,256]{2,1,0:T(8,128)S(1)}, f32[2,8,256]{2,1,0:T(8,128)}, u32[]{:S(2)}) copy-start(f32[2,8,256]{2,1,0:T(8,128)} %direction_ref.7) | copy-start | bytes 49156
  75.0 21.0 %copy-start.5 = (f32[2,8,256]{2,1,0:T(8,128)S(1)}, f32[2,8,256]{2,1,0:T(8,128)}, u32[]{:S(2)}) copy-start(f32[2,8,256]{2,1,0:T(8,128)} %residual_ref.3) | copy-start | bytes 49156
  75.1 20.9 %copy-start = (f32[2,4,256,256]{3,2,1,0:T(8,128)S(1)}, f32[2,4,256,256]{3,2,1,0:T(8,128)}, u32[]{:S(2)}) copy-start(f32[2,4,256,256]{3,2,1,0:T(8,128)} %far_cross.3) | copy-start | bytes 6291460
  96.0 1.6 copy-start.1
  100.1 31.4 %copy-start.6 = (f32[2,8,256]{2,1,0:T(8,128)S(1)}, f32[2,8,256]{2,1,0:T(8,128)}, u32[]{:S(2)}) copy-start(f32[2,8,256]{2,1,0:T(8,128)} %solution_ref.1) | copy-start | bytes 49156
  128.3 3.2 %collective-permute-start.7 = (f32[64,5,8,128]{3,2,1,0:T(8,128)S(1)}, f32[64,5,8,128]{3,2,1,0:T(8,128)}, u32[]{:S(2)}, u32[]{:S(2)}) collective-permute-start(f32[64,5,8,128]{3,2,1,0:T(8,128)S(1)} %all_to_all.16.mine_ref), channel_id=1, source_target_pairs={{0,1},{1,0},{2,3},{3,2},{4,5},{5,4},{6,7},{7,6},{8,9},{9,8},{10,11... | collective-permute-start | bytes 3932168 | tf_op jit(solution)/shard_map/ppermute | solution.py:450
  131.4 1.0 copy-start.3
  138.1 3.1 %collective-permute-start.8 = (f32[64,5,8,128]{3,2,1,0:T(8,128)S(1)}, f32[64,5,8,128]{3,2,1,0:T(8,128)S(1)}, u32[]{:S(2)}, u32[]{:S(2)}) collective-permute-start(f32[64,5,8,128]{3,2,1,0:T(8,128)S(1)} %slice.7), channel_id=1, source_target_pairs={{0,1},{1,0},{2,3},{3,2},{4,5},{5,4},{6,7},{7,6},{8,9},{9,8},{10,11... | collective-permute-start | bytes 3932168 | tf_op jit(solution)/shard_map/ppermute | solution.py:450
Sparse Core Ops, SparseCore 0:
  11.2 73.1 all-gather.1
